TPU v7x, 512 devices: a whole 4x4x16 slice. The times are simulated.
512 devices in a mesh: win: 64 (over y, z), state: 8 (over x, core).
Axes of the slice: x: 4, y: 4, z: 16, core: 2. Of those that a mesh axis runs over, the one named last changes fastest.
Arguments:
- anomalies: float32 [64, 2048, 256], P('win', 'state'), may hold values from -12 to 12
- mean_state: float32 [64, 2048], P('win', 'state'), may hold values from -6 to 6
- obs_rows: int32 [64, 1024], P('win', 'state'), may hold values from 0 to 255
- obs_precision: float32 [64, 1024], P('win', 'state'), may hold values from 0.001953125 to 0.01953125
Outputs:
- updated: float32 [64, 2048, 256], P('win', 'state')
Inputs may be any that keep to these rules, and one draw needn't show every extreme that they name: Observation j of window w reads state row (j // 128) * 256 + obs_rows[w, j], a row of the same block of 256 rows.
All inputs are finite; a program needn't handle non-finite values.
Results may differ from a plain program's by a relative error of at most 0.0003.
Values sent between devices are 32-bit elements; how exact they have to be, the bound alone decides.
No kernel may reach another device: no remote copies, remote signals or barrier semaphores. Data moves between devices by JAX's collectives and lax.ppermute only.
A program may use at most 128 MiB of HBM per device.

v0:
```python
import functools

import jax
import jax.numpy as jnp
from jax import lax
from jax.experimental import pallas as pl
from jax.experimental.pallas import tpu as pltpu
from jax.sharding import Mesh, PartitionSpec as P


F32 = jnp.float32
BF16 = jnp.bfloat16
N = 256
H = 128
PACK = 272
NS_STEPS = 3
WIDE, THIN = N // 4, N // 8
VMEM_BYTES = 8 * 1024 * 1024


def split(a):
    hi = a.astype(BF16)
    lo = (a - hi.astype(F32)).astype(BF16)
    return hi, lo


def mm(a, b):
    dot = functools.partial(jnp.dot, preferred_element_type=F32)
    return dot(a[0], b[0]) + (dot(a[0], b[1]) + dot(a[1], b[0]))


def eye_mask(n):
    i = lax.broadcasted_iota(jnp.int32, (n, n), 0)
    j = lax.broadcasted_iota(jnp.int32, (n, n), 1)
    return i, j


def column(row, n):
    i, j = eye_mask(n)
    return jnp.sum(jnp.where(i == j, row, 0.0), axis=1, keepdims=True)


def pack(m, out):
    i, j = eye_mask(H)
    first, corner = m[:H, :H], m[H:, H:]
    rows = jnp.where(i <= j, first, corner)
    diag = jnp.sum(jnp.where(i == j, corner, 0.0), axis=0, keepdims=True)
    tail = jnp.where(lax.broadcasted_iota(jnp.int32, (PACK - N, H), 0) == 0, diag, 0.0)
    out[:H, :] = rows
    out[H:N, :] = m[:H, H:]
    out[N:, :] = tail


def unpack(p):
    i, j = eye_mask(H)
    rows, cross, diag = p[:H], p[H:N], p[N:N + 1]
    turned = rows.T
    first = jnp.where(i <= j, rows, turned)
    corner = jnp.where(i > j, rows, jnp.where(i < j, turned, diag))
    top = jnp.concatenate([first, cross], axis=1)
    low = jnp.concatenate([cross.T, corner], axis=1)
    return jnp.concatenate([top, low], axis=0)


def gram_kernel(*refs):
    sources, out_ref, held, sems = refs[:4], refs[4], refs[5:9], refs[9]
    copies = [
        pltpu.make_async_copy(source, target, sems.at[place])
        for place, (source, target) in enumerate(zip(sources, held))
    ]
    for copy in copies:
        copy.start()
    for copy in copies:
        copy.wait()
    cur_ref, mean_ref, rows_ref, prec_ref = held
    value = cur_ref[...] + column(mean_ref[...], N)
    state_row = lax.broadcasted_iota(jnp.int32, (N, H), 0)
    chosen = (state_row == rows_ref[...]).astype(F32).T.astype(BF16)
    dot = functools.partial(jnp.dot, preferred_element_type=F32)
    one = value.astype(BF16)
    rest = value - one.astype(F32)
    two = rest.astype(BF16)
    three = (rest - two.astype(F32)).astype(BF16)
    picked = dot(chosen, one) + (dot(chosen, two) + dot(chosen, three))
    predicted = jnp.tanh(picked)
    centred = predicted - jnp.mean(predicted, axis=1, keepdims=True)
    centred = centred * jnp.sqrt(column(prec_ref[...], H))
    gram = mm(split(centred.T), split(centred)) * (1.0 / (N - 1))
    pack(gram, out_ref)


def root_kernel(parts_ref, out_ref, packed):
    total = (parts_ref[0] + parts_ref[1]) + (parts_ref[2] + parts_ref[3])
    i, j = eye_mask(N)
    unit = jnp.where(i == j, 1.0, 0.0)
    system = unpack(total) + unit
    square = jnp.sum(jnp.sum(system * system, axis=0, keepdims=True), axis=1, keepdims=True)
    root = system * (1.0 / jnp.sqrt(square))
    factor = 1.5 * unit - 0.5 * root
    inverse = split(factor)
    root = split(mm(split(root), inverse))
    for step in range(1, NS_STEPS):
        factor = split(1.5 * unit - 0.5 * mm(inverse, root))
        if step + 1 < NS_STEPS:
            root = split(mm(root, factor))
        last = mm(factor, inverse)
        inverse = split(last)
    diag = jnp.where(i == j, last, 0.0)
    trace = jnp.sum(jnp.sum(diag, axis=0, keepdims=True), axis=1, keepdims=True)
    pack(last * (N / trace), packed)
    core = lax.axis_index("core")
    half = packed[pl.ds(pl.multiple_of(core * (PACK // 2), 8), PACK // 2), :]
    for copy in range(4):
        out_ref[copy] = half


def transforms(parts_ref):
    out = []
    for place in range(4):
        out.append(unpack(jnp.concatenate([parts_ref[0, place], parts_ref[1, place]], axis=0)))
    return out


def slices(total_ref, wide_ref, thin_ref):
    chip = lax.axis_index("x")
    core = lax.axis_index("core")
    wide_ref[...] = total_ref[pl.ds(pl.multiple_of(chip * WIDE, 8), WIDE), :]
    thin_ref[...] = total_ref[pl.ds(pl.multiple_of(core * H + chip * THIN, 8), THIN), :]


def quad_kernel(parts_ref, total_ref, wide_ref, thin_ref):
    one, two, three, four = [split(t) for t in transforms(parts_ref)]
    total_ref[...] = mm(split(mm(one, two)), split(mm(three, four)))
    slices(total_ref, wide_ref, thin_ref)


def quad_apply_kernel(parts_ref, cur_ref, out_ref):
    mine = lax.axis_index("zl")
    out_ref[...] = cur_ref[...]
    for place in range(4):

        @pl.when(place >= mine)
        def _():
            t = unpack(jnp.concatenate([parts_ref[0, place], parts_ref[1, place]], axis=0))
            out_ref[...] = mm(split(out_ref[...]), split(t))


def joined(ring_ref):
    after = ring_ref[0, :, :WIDE].reshape(N, N)
    before = ring_ref[1, :, :WIDE].reshape(N, N)
    across = [ring_ref[core, :, WIDE:].reshape(H, N) for core in range(2)]
    return after, jnp.concatenate(across, axis=0), before


def ring_kernel(ring_ref, mine_ref, total_ref, half_ref, one, two):
    quad = lax.axis_index("zh")
    mine = split(mine_ref[...])
    after, across, before = [split(m) for m in joined(ring_ref)]

    @pl.when(quad % 2 == 0)
    def _():
        one[...] = mm(mine, after)
        two[...] = mm(across, before)

    @pl.when(quad % 2 == 1)
    def _():
        one[...] = mm(before, mine)
        two[...] = mm(after, across)

    @pl.when(quad < 2)
    def _():
        total_ref[...] = mm(split(one[...]), split(two[...]))

    @pl.when(quad >= 2)
    def _():
        total_ref[...] = mm(split(two[...]), split(one[...]))

    core = lax.axis_index("core")
    half_ref[...] = total_ref[pl.ds(pl.multiple_of(core * H, 8), H), :]


def ring_apply_kernel(ring_ref, cur_ref, out_ref):
    quad = lax.axis_index("zh")
    out_ref[...] = cur_ref[...]
    for place, later in enumerate(joined(ring_ref)):

        @pl.when(quad + place < 3)
        def _():
            out_ref[...] = mm(split(out_ref[...]), split(later))


def row_apply_kernel(near_ref, cur_ref, out_ref):
    row = lax.axis_index("y")
    out_ref[...] = cur_ref[...]

    @pl.when(row < 3)
    def _():
        out_ref[...] = mm(split(out_ref[...]), split(near_ref[0, :N]))

    @pl.when(row < 2)
    def _():
        second = jnp.concatenate([near_ref[0, N:], near_ref[1, N:]], axis=0)
        out_ref[...] = mm(split(out_ref[...]), split(second))

    @pl.when(row < 1)
    def _():
        out_ref[...] = mm(split(out_ref[...]), split(near_ref[1, :N]))


VMEM = pl.BlockSpec(memory_space=pltpu.VMEM)


def call(kernel, outs, args, products, scratch=(), space=VMEM, limit=VMEM_BYTES):
    many = isinstance(outs, list)
    shapes = [jax.ShapeDtypeStruct(s, F32) for s in (outs if many else [outs])]
    moved = sum(a.size * 4 for a in args) + sum(s.size * 4 for s in shapes)
    return pl.pallas_call(
        kernel,
        out_shape=shapes if many else shapes[0],
        in_specs=[space] * len(args),
        out_specs=[VMEM] * len(shapes) if many else VMEM,
        scratch_shapes=list(scratch),
        compiler_params=pltpu.CompilerParams(vmem_limit_bytes=limit),
        cost_estimate=pl.CostEstimate(
            flops=products * 6 * N * N * N, bytes_accessed=moved, transcendentals=0
        ),
    )(*args)


RING = 16
NEAR = [
    (2 * z + core, 2 * ((z + step) % RING) + core)
    for core, step in enumerate((-4, 4))
    for z in range(RING)
]
ACROSS = [(z, (11 - z) if z % 8 < 4 else (19 - z)) for z in range(RING)]


def from_later(steps):
    return [
        (2 * row + core, 2 * (row - back) + core)
        for core, back in enumerate(steps)
        for row in range(back, 4)
    ]


ROW_ODD = from_later((1, 3))
ROW_EVEN = [(row, row - 2) for row in range(2, 4)]


def smoother(anomalies, mean_state, obs_rows, obs_precision):
    current = anomalies[0]
    sources = (current, mean_state, obs_rows, obs_precision)
    gram = call(
        gram_kernel,
        (PACK, H),
        [pltpu.with_memory_space_constraint(a, pltpu.HBM) for a in sources],
        1,
        [pltpu.VMEM(a.shape, a.dtype) for a in sources] + [pltpu.SemaphoreType.DMA((4,))],
        pl.BlockSpec(memory_space=pltpu.HBM),
    )
    both = lax.all_gather(gram, "core")
    spread = jnp.broadcast_to(both[0] + both[1], (4, PACK, H))
    parts = lax.all_to_all(spread, "x", 0, 0)
    half = call(root_kernel, (4, PACK // 2, H), (parts,), 6, [pltpu.VMEM((PACK, H), F32)])
    parts = lax.all_gather(lax.all_to_all(half, "zl", 0, 0), "core")
    full = (N, N)
    wide, thin = (WIDE, N), (THIN, N)
    total, wide, thin = call(quad_kernel, [full, wide, thin], (parts,), 3)
    current = call(quad_apply_kernel, full, (parts, current), 4)
    across = lax.ppermute(thin, ("zh", "zl"), ACROSS)
    near = lax.ppermute(wide, ("zh", "zl", "core"), NEAR)
    piece = jnp.concatenate([near, across], axis=0)
    piece = jnp.broadcast_to(piece, (4, WIDE + THIN, N))
    ring = lax.all_gather(lax.all_to_all(piece, "x", 0, 0), "core")
    square = pltpu.VMEM(full, F32)
    total, half = call(ring_kernel, [full, (H, N)], (ring, total), 3, [square, square])
    current = call(ring_apply_kernel, full, (ring, current), 3)
    near = lax.ppermute(total, ("y", "core"), ROW_ODD)
    across = lax.ppermute(half, "y", ROW_EVEN)
    near = lax.all_gather(jnp.concatenate([near, across], axis=0), "core")
    return call(row_apply_kernel, full, (near, current), 3)[None]


def solution(mesh):
    devices = mesh.devices.reshape(4, 4, 4, 4, 2)
    grid = Mesh(devices, ("y", "zh", "zl", "x", "core"))
    win, state = ("y", "zh", "zl"), ("x", "core")
    placed = (P(win, state, None), P(win, state), P(win, state), P(win, state))
    return jax.shard_map(
        smoother, mesh=grid, in_specs=placed, out_specs=P(win, state, None), check_vma=False
    )
```

profile of v0, /device:TPU:1, one launch (start us, length us, event | category | flops | bytes accessed | tf_op | source)
XLA Modules:
  0.0 88.5 jit_solution(1143861300043005365)
XLA Ops:
  0.0 1.8 %shard_map.46 = f32[272,128]{1,0:T(8,128)S(1)} custom-call(f32[256,256]{1,0:T(8,128)} %bitcast.10, f32[1,256]{1,0:T(1,128)} %refs_1_.1, s32[1,128]{1,0:T(1,128)} %refs_2_.1, f32[1,128]{1,0:T(1,128)} %refs_3_.1), custom_call_target="tpu_custom_call" | custom-call | flops 100663296 | bytes 403456 | tf_op jit(solution)/shard_map/pallas_call | solution.py:217
  1.8 8.5 %all-gather = f32[544,128]{1,0:T(8,128)S(1)} all-gather(f32[272,128]{1,0:T(8,128)S(1)} %shard_map.46), channel_id=2, replica_groups=mesh['y'=4,'zh'=4,'zl'=4,'x'=4,'core'=2] {'core'}, dimensions={0}, use_global_device_ids=true | all-gather | bytes 417792 | tf_op jit(solution)/shard_map/all_gather | solution.py:262
  10.3 11.8 %all_to_all.15.parts_ref = f32[4,272,128]{2,1,0:T(8,128)S(1)} all-to-all(f32[4,272,128]{2,1,0:T(8,128)S(1)} %broadcast_in_dim.9), channel_id=1, replica_groups=mesh['y'=4,'zh'=4,'zl'=4,'x'=4,'core'=2] {'x'}, dimensions={0} | all-to-all | bytes 1114112 | tf_op jit(solution)/shard_map/all_to_all | solution.py:264
  22.2 1.9 %shard_map.47 = f32[4,136,128]{2,1,0:T(8,128)S(1)} custom-call(f32[4,272,128]{2,1,0:T(8,128)S(1)} %all_to_all.15.parts_ref), custom_call_target="tpu_custom_call" | custom-call | flops 603979776 | bytes 835584 | tf_op jit(solution)/shard_map/pallas_call | solution.py:217
  24.1 9.6 %all_to_all.16 = f32[4,136,128]{2,1,0:T(8,128)S(1)} all-to-all(f32[4,136,128]{2,1,0:T(8,128)S(1)} %shard_map.47), channel_id=1, replica_groups=mesh['y'=4,'zh'=4,'zl'=4,'x'=4,'core'=2] {'zl'}, dimensions={0} | all-to-all | bytes 557056 | tf_op jit(solution)/shard_map/all_to_all | solution.py:266
  33.7 4.8 %all-gather.1 = f32[8,136,128]{2,1,0:T(8,128)S(1)} all-gather(f32[4,136,128]{2,1,0:T(8,128)S(1)} %all_to_all.16), channel_id=3, replica_groups=mesh['y'=4,'zh'=4,'zl'=4,'x'=4,'core'=2] {'core'}, dimensions={0}, use_global_device_ids=true | all-gather | bytes 835584 | tf_op jit(solution)/shard_map/all_gather | solution.py:266
  38.5 0.9 %shard_map.48 = (f32[256,256]{1,0:T(8,128)S(1)}, f32[64,256]{1,0:T(8,128)S(1)}, f32[32,256]{1,0:T(8,128)S(1)}) custom-call(f32[2,4,136,128]{3,2,1,0:T(8,128)S(1)} %bitcast.8), custom_call_target="tpu_custom_call" | custom-call | flops 301989888 | bytes 917504 | tf_op jit(solution)/shard_map/pallas_call | solution.py:217
  39.4 7.8 %collective-permute-start = (f32[64,256]{1,0:T(8,128)S(1)}, f32[64,256]{1,0:T(8,128)S(1)}, u32[]{:S(2)}, u32[]{:S(2)}) collective-permute-start(f32[64,256]{1,0:T(8,128)S(1)} %get-tuple-element.10), channel_id=1, source_target_pairs={{0,96},{8,104},{16,112},{24,120},{32,0},{40,8},{48,16},{56,24},{64... | collective-permute-start | bytes 196616 | tf_op jit(solution)/shard_map/ppermute | solution.py:272
  47.2 6.1 %collective-permute-start.1 = (f32[32,256]{1,0:T(8,128)S(1)}, f32[32,256]{1,0:T(8,128)S(1)}, u32[]{:S(2)}, u32[]{:S(2)}) collective-permute-start(f32[32,256]{1,0:T(8,128)S(1)} %get-tuple-element.11), channel_id=1, source_target_pairs={{0,88},{8,80},{16,72},{24,64},{32,120},{40,112},{48,104},{56,96},{... | collective-permute-start | bytes 98312 | tf_op jit(solution)/shard_map/ppermute | solution.py:271
  53.3 4.6 %collective-permute-done.1 = f32[32,256]{1,0:T(8,128)S(1)} collective-permute-done((f32[32,256]{1,0:T(8,128)S(1)}, f32[32,256]{1,0:T(8,128)S(1)}, u32[]{:S(2)}, u32[]{:S(2)}) %collective-permute-start.1) | collective-permute-done | bytes 32800 | tf_op jit(solution)/shard_map/ppermute | solution.py:271
  58.0 0.0 collective-permute-done
  58.0 8.6 %all_to_all.17 = f32[4,96,256]{2,1,0:T(8,128)S(1)} all-to-all(f32[4,96,256]{2,1,0:T(8,128)S(1)} %broadcast_in_dim.10), channel_id=1, replica_groups=mesh['y'=4,'zh'=4,'zl'=4,'x'=4,'core'=2] {'x'}, dimensions={0} | all-to-all | bytes 786432 | tf_op jit(solution)/shard_map/all_to_all | solution.py:275
  66.6 5.9 %all-gather.2 = f32[8,96,256]{2,1,0:T(8,128)S(1)} all-gather(f32[4,96,256]{2,1,0:T(8,128)S(1)} %all_to_all.17), channel_id=4, replica_groups=mesh['y'=4,'zh'=4,'zl'=4,'x'=4,'core'=2] {'core'}, dimensions={0}, use_global_device_ids=true | all-gather | bytes 1179648 | tf_op jit(solution)/shard_map/all_gather | solution.py:275
  72.5 0.0 copy-start
  72.5 0.8 shard_map.49
  73.4 1.3 %collective-permute-start.2 = (f32[256,256]{1,0:T(8,128)S(1)}, f32[256,256]{1,0:T(8,128)S(1)}, u32[]{:S(2)}, u32[]{:S(2)}) collective-permute-start(f32[256,256]{1,0:T(8,128)S(1)} %get-tuple-element.13), channel_id=1, source_target_pairs={{128,0},{256,128},{384,256},{385,1},{130,2},{258,130},{386,258},{3... | collective-permute-start | bytes 786440 | tf_op jit(solution)/shard_map/ppermute | solution.py:279
  74.7 1.3 %collective-permute-start.3 = (f32[128,256]{1,0:T(8,128)S(1)}, f32[128,256]{1,0:T(8,128)S(1)}, u32[]{:S(2)}, u32[]{:S(2)}) collective-permute-start(f32[128,256]{1,0:T(8,128)S(1)} %get-tuple-element.14), channel_id=1, source_target_pairs={{256,0},{384,128},{257,1},{385,129},{258,2},{386,130},{259,3},{387... | collective-permute-start | bytes 393224 | tf_op jit(solution)/shard_map/ppermute | solution.py:280
  76.0 0.0 copy-done
  76.0 1.5 %shard_map.50.cur_ref = f32[256,256]{1,0:T(8,128)S(1)} custom-call(f32[2,4,136,128]{3,2,1,0:T(8,128)S(1)} %bitcast.9, f32[256,256]{1,0:T(8,128)S(1)} %bitcast.11), custom_call_target="tpu_custom_call" | custom-call | flops 402653184 | bytes 1081344 | tf_op jit(solution)/shard_map/pallas_call | solution.py:217
  77.5 0.9 %shard_map.51.cur_ref = f32[256,256]{1,0:T(8,128)S(1)} custom-call(f32[2,4,96,256]{3,2,1,0:T(8,128)S(1)} %bitcast.6, f32[256,256]{1,0:T(8,128)S(1)} %shard_map.50.cur_ref), custom_call_target="tpu_custom_call" | custom-call | flops 301989888 | bytes 1310720 | tf_op jit(solution)/shard_map/pallas_call | solution.py:217
  78.4 4.3 %collective-permute-done.3 = f32[128,256]{1,0:T(8,128)S(1)} collective-permute-done((f32[128,256]{1,0:T(8,128)S(1)}, f32[128,256]{1,0:T(8,128)S(1)}, u32[]{:S(2)}, u32[]{:S(2)}) %collective-permute-start.3) | collective-permute-done | bytes 131104 | tf_op jit(solution)/shard_map/ppermute | solution.py:280
  82.7 1.8 %collective-permute-done.2 = f32[256,256]{1,0:T(8,128)S(1)} collective-permute-done((f32[256,256]{1,0:T(8,128)S(1)}, f32[256,256]{1,0:T(8,128)S(1)}, u32[]{:S(2)}, u32[]{:S(2)}) %collective-permute-start.2) | collective-permute-done | bytes 262176 | tf_op jit(solution)/shard_map/ppermute | solution.py:279
  84.5 2.4 %all-gather.3 = f32[768,256]{1,0:T(8,128)S(1)} all-gather(f32[384,256]{1,0:T(8,128)S(1)} %pad_maximum_fusion), channel_id=5, replica_groups=mesh['y'=4,'zh'=4,'zl'=4,'x'=4,'core'=2] {'core'}, dimensions={0}, use_global_device_ids=true | all-gather | bytes 1179648 | tf_op jit(solution)/shard_map/all_gather | solution.py:281
  86.9 1.6 %shard_map.52 = f32[256,256]{1,0:T(8,128)} custom-call(f32[2,384,256]{2,1,0:T(8,128)S(1)} %bitcast.7, f32[256,256]{1,0:T(8,128)S(1)} %shard_map.51.cur_ref), custom_call_target="tpu_custom_call" | custom-call | flops 301989888 | bytes 1310720 | tf_op jit(solution)/shard_map/pallas_call | solution.py:217
  (5 shorter events, 0.1 us)
Async XLA Ops:
  39.4 18.6 %collective-permute-start = (f32[64,256]{1,0:T(8,128)S(1)}, f32[64,256]{1,0:T(8,128)S(1)}, u32[]{:S(2)}, u32[]{:S(2)}) collective-permute-start(f32[64,256]{1,0:T(8,128)S(1)} %get-tuple-element.10), channel_id=1, source_target_pairs={{0,96},{8,104},{16,112},{24,120},{32,0},{40,8},{48,16},{56,24},{64... | collective-permute-start | bytes 196616 | tf_op jit(solution)/shard_map/ppermute | solution.py:272
  47.2 10.8 %collective-permute-start.1 = (f32[32,256]{1,0:T(8,128)S(1)}, f32[32,256]{1,0:T(8,128)S(1)}, u32[]{:S(2)}, u32[]{:S(2)}) collective-permute-start(f32[32,256]{1,0:T(8,128)S(1)} %get-tuple-element.11), channel_id=1, source_target_pairs={{0,88},{8,80},{16,72},{24,64},{32,120},{40,112},{48,104},{56,96},{... | collective-permute-start | bytes 98312 | tf_op jit(solution)/shard_map/ppermute | solution.py:271
  72.5 3.4 %copy-start = (f32[1,256,256]{2,1,0:T(8,128)S(1)}, f32[1,256,256]{2,1,0:T(8,128)}, u32[]{:S(2)}) copy-start(f32[1,256,256]{2,1,0:T(8,128)} %param.4) | copy-start | bytes 786436
  73.4 11.1 %collective-permute-start.2 = (f32[256,256]{1,0:T(8,128)S(1)}, f32[256,256]{1,0:T(8,128)S(1)}, u32[]{:S(2)}, u32[]{:S(2)}) collective-permute-start(f32[256,256]{1,0:T(8,128)S(1)} %get-tuple-element.13), channel_id=1, source_target_pairs={{128,0},{256,128},{384,256},{385,1},{130,2},{258,130},{386,258},{3... | collective-permute-start | bytes 786440 | tf_op jit(solution)/shard_map/ppermute | solution.py:279
  74.7 8.0 %collective-permute-start.3 = (f32[128,256]{1,0:T(8,128)S(1)}, f32[128,256]{1,0:T(8,128)S(1)}, u32[]{:S(2)}, u32[]{:S(2)}) collective-permute-start(f32[128,256]{1,0:T(8,128)S(1)} %get-tuple-element.14), channel_id=1, source_target_pairs={{256,0},{384,128},{257,1},{385,129},{258,2},{386,130},{259,3},{387... | collective-permute-start | bytes 393224 | tf_op jit(solution)/shard_map/ppermute | solution.py:280
where the time goes:
time: 89 us; the launch traced here: 88.5 us
  blocking collectives  51.5 us (58%)
  starting transfers between devices  16.5 us (19%)
  waiting for transfers between devices  10.8 us (12%)
  Pallas kernels  9.4 us (11%)
    all_to_all x1, blocking collectives, smoother(): parts = lax.all_to_all(spread, 'x', 0, 0)  11.8 us
    all_to_all x1, blocking collectives, smoother(): parts = lax.all_gather(lax.all_to_all(half, 'zl', 0, 0), 'core')  9.56 us
    pallas_call x7, Pallas kernels, call(): pl.pallas_call(kernel, out_shape=shapes if many else shapes[0], in_specs=...  9.4 us
    all_to_all x1, blocking collectives, smoother(): ring = lax.all_gather(lax.all_to_all(piece, 'x', 0, 0), 'core')  8.62 us
    all_gather x1, blocking collectives, smoother(): both = lax.all_gather(gram, 'core')  8.48 us
    ppermute x1, starting transfers between devices, smoother(): near = lax.ppermute(wide, ('zh', 'zl', 'core'), NEAR)  7.8 us
    ppermute x1, starting transfers between devices, smoother(): across = lax.ppermute(thin, ('zh', 'zl'), ACROSS)  6.14 us
    all_gather x1, blocking collectives, smoother(): ring = lax.all_gather(lax.all_to_all(piece, 'x', 0, 0), 'core')  5.89 us
  transfers between devices with their start and end apart: 4, of which 3 were waited for; matrix products, arithmetic and copies ran while one was open for 0% of the time, Pallas kernels for 3%

commit v1 on v0

--- a/solution.py
+++ b/solution.py
@@ -191,20 +191,26 @@
 
 def row_apply_kernel(near_ref, cur_ref, out_ref):
     row = lax.axis_index("y")
-    out_ref[...] = cur_ref[...]
-
-    @pl.when(row < 3)
-    def _():
-        out_ref[...] = mm(split(out_ref[...]), split(near_ref[0, :N]))
-
-    @pl.when(row < 2)
-    def _():
-        second = jnp.concatenate([near_ref[0, N:], near_ref[1, N:]], axis=0)
-        out_ref[...] = mm(split(out_ref[...]), split(second))
-
-    @pl.when(row < 1)
-    def _():
-        out_ref[...] = mm(split(out_ref[...]), split(near_ref[1, :N]))
+    second = jnp.concatenate([near_ref[0, N:], near_ref[1, N:]], axis=0)
+
+    @pl.when(row == 0)
+    def _():
+        later = mm(split(second), split(near_ref[1, :N]))
+        first = mm(split(cur_ref[...]), split(near_ref[0, :N]))
+        out_ref[...] = mm(split(first), split(later))
+
+    @pl.when(row == 1)
+    def _():
+        first = mm(split(cur_ref[...]), split(near_ref[0, :N]))
+        out_ref[...] = mm(split(first), split(second))
+
+    @pl.when(row == 2)
+    def _():
+        out_ref[...] = mm(split(cur_ref[...]), split(near_ref[0, :N]))
+
+    @pl.when(row == 3)
+    def _():
+        out_ref[...] = cur_ref[...]
 
 
 VMEM = pl.BlockSpec(memory_space=pltpu.VMEM)

time: 89 us -> 89 us (level)
  no operation moved by 1% of the time
where the time goes in v1:
time: 89 us; the launch traced here: 88.4 us
  blocking collectives  51.5 us (58%)
  starting transfers between devices  16.5 us (19%)
  waiting for transfers between devices  10.8 us (12%)
  Pallas kernels  9.31 us (10%)
    all_to_all x1, blocking collectives, smoother(): parts = lax.all_to_all(spread, 'x', 0, 0)  11.8 us
    all_to_all x1, blocking collectives, smoother(): parts = lax.all_gather(lax.all_to_all(half, 'zl', 0, 0), 'core')  9.56 us
    pallas_call x7, Pallas kernels, call(): pl.pallas_call(kernel, out_shape=shapes if many else shapes[0], in_specs=...  9.31 us
    all_to_all x1, blocking collectives, smoother(): ring = lax.all_gather(lax.all_to_all(piece, 'x', 0, 0), 'core')  8.62 us
    all_gather x1, blocking collectives, smoother(): both = lax.all_gather(gram, 'core')  8.48 us
    ppermute x1, starting transfers between devices, smoother(): near = lax.ppermute(wide, ('zh', 'zl', 'core'), NEAR)  7.8 us
    ppermute x1, starting transfers between devices, smoother(): across = lax.ppermute(thin, ('zh', 'zl'), ACROSS)  6.14 us
    all_gather x1, blocking collectives, smoother(): ring = lax.all_gather(lax.all_to_all(piece, 'x', 0, 0), 'core')  5.89 us
  transfers between devices with their start and end apart: 4, of which 3 were waited for; matrix products, arithmetic and copies ran while one was open for 0% of the time, Pallas kernels for 3%

profile of v1, /device:TPU:1, one launch (start us, length us, event | category | flops | bytes accessed | tf_op | source)
XLA Modules:
  0.0 88.4 jit_solution(5711125779601861270)
XLA Ops:
  0.0 1.8 %shard_map.46 = f32[272,128]{1,0:T(8,128)S(1)} custom-call(f32[256,256]{1,0:T(8,128)} %bitcast.10, f32[1,256]{1,0:T(1,128)} %refs_1_.1, s32[1,128]{1,0:T(1,128)} %refs_2_.1, f32[1,128]{1,0:T(1,128)} %refs_3_.1), custom_call_target="tpu_custom_call" | custom-call | flops 100663296 | bytes 403456 | tf_op jit(solution)/shard_map/pallas_call | solution.py:223
  1.8 8.5 %all-gather = f32[544,128]{1,0:T(8,128)S(1)} all-gather(f32[272,128]{1,0:T(8,128)S(1)} %shard_map.46), channel_id=2, replica_groups=mesh['y'=4,'zh'=4,'zl'=4,'x'=4,'core'=2] {'core'}, dimensions={0}, use_global_device_ids=true | all-gather | bytes 417792 | tf_op jit(solution)/shard_map/all_gather | solution.py:268
  10.3 11.8 %all_to_all.15.parts_ref = f32[4,272,128]{2,1,0:T(8,128)S(1)} all-to-all(f32[4,272,128]{2,1,0:T(8,128)S(1)} %broadcast_in_dim.9), channel_id=1, replica_groups=mesh['y'=4,'zh'=4,'zl'=4,'x'=4,'core'=2] {'x'}, dimensions={0} | all-to-all | bytes 1114112 | tf_op jit(solution)/shard_map/all_to_all | solution.py:270
  22.2 1.9 %shard_map.47 = f32[4,136,128]{2,1,0:T(8,128)S(1)} custom-call(f32[4,272,128]{2,1,0:T(8,128)S(1)} %all_to_all.15.parts_ref), custom_call_target="tpu_custom_call" | custom-call | flops 603979776 | bytes 835584 | tf_op jit(solution)/shard_map/pallas_call | solution.py:223
  24.1 9.6 %all_to_all.16 = f32[4,136,128]{2,1,0:T(8,128)S(1)} all-to-all(f32[4,136,128]{2,1,0:T(8,128)S(1)} %shard_map.47), channel_id=1, replica_groups=mesh['y'=4,'zh'=4,'zl'=4,'x'=4,'core'=2] {'zl'}, dimensions={0} | all-to-all | bytes 557056 | tf_op jit(solution)/shard_map/all_to_all | solution.py:272
  33.7 4.8 %all-gather.1 = f32[8,136,128]{2,1,0:T(8,128)S(1)} all-gather(f32[4,136,128]{2,1,0:T(8,128)S(1)} %all_to_all.16), channel_id=3, replica_groups=mesh['y'=4,'zh'=4,'zl'=4,'x'=4,'core'=2] {'core'}, dimensions={0}, use_global_device_ids=true | all-gather | bytes 835584 | tf_op jit(solution)/shard_map/all_gather | solution.py:272
  38.5 0.9 %shard_map.48 = (f32[256,256]{1,0:T(8,128)S(1)}, f32[64,256]{1,0:T(8,128)S(1)}, f32[32,256]{1,0:T(8,128)S(1)}) custom-call(f32[2,4,136,128]{3,2,1,0:T(8,128)S(1)} %bitcast.8), custom_call_target="tpu_custom_call" | custom-call | flops 301989888 | bytes 917504 | tf_op jit(solution)/shard_map/pallas_call | solution.py:223
  39.4 7.8 %collective-permute-start = (f32[64,256]{1,0:T(8,128)S(1)}, f32[64,256]{1,0:T(8,128)S(1)}, u32[]{:S(2)}, u32[]{:S(2)}) collective-permute-start(f32[64,256]{1,0:T(8,128)S(1)} %get-tuple-element.10), channel_id=1, source_target_pairs={{0,96},{8,104},{16,112},{24,120},{32,0},{40,8},{48,16},{56,24},{64... | collective-permute-start | bytes 196616 | tf_op jit(solution)/shard_map/ppermute | solution.py:278
  47.2 6.1 %collective-permute-start.1 = (f32[32,256]{1,0:T(8,128)S(1)}, f32[32,256]{1,0:T(8,128)S(1)}, u32[]{:S(2)}, u32[]{:S(2)}) collective-permute-start(f32[32,256]{1,0:T(8,128)S(1)} %get-tuple-element.11), channel_id=1, source_target_pairs={{0,88},{8,80},{16,72},{24,64},{32,120},{40,112},{48,104},{56,96},{... | collective-permute-start | bytes 98312 | tf_op jit(solution)/shard_map/ppermute | solution.py:277
  53.3 4.6 %collective-permute-done.1 = f32[32,256]{1,0:T(8,128)S(1)} collective-permute-done((f32[32,256]{1,0:T(8,128)S(1)}, f32[32,256]{1,0:T(8,128)S(1)}, u32[]{:S(2)}, u32[]{:S(2)}) %collective-permute-start.1) | collective-permute-done | bytes 32800 | tf_op jit(solution)/shard_map/ppermute | solution.py:277
  58.0 0.0 collective-permute-done
  58.0 8.6 %all_to_all.17 = f32[4,96,256]{2,1,0:T(8,128)S(1)} all-to-all(f32[4,96,256]{2,1,0:T(8,128)S(1)} %broadcast_in_dim.10), channel_id=1, replica_groups=mesh['y'=4,'zh'=4,'zl'=4,'x'=4,'core'=2] {'x'}, dimensions={0} | all-to-all | bytes 786432 | tf_op jit(solution)/shard_map/all_to_all | solution.py:281
  66.6 5.9 %all-gather.2 = f32[8,96,256]{2,1,0:T(8,128)S(1)} all-gather(f32[4,96,256]{2,1,0:T(8,128)S(1)} %all_to_all.17), channel_id=4, replica_groups=mesh['y'=4,'zh'=4,'zl'=4,'x'=4,'core'=2] {'core'}, dimensions={0}, use_global_device_ids=true | all-gather | bytes 1179648 | tf_op jit(solution)/shard_map/all_gather | solution.py:281
  72.5 0.0 copy-start
  72.5 0.8 shard_map.49
  73.4 1.3 %collective-permute-start.2 = (f32[256,256]{1,0:T(8,128)S(1)}, f32[256,256]{1,0:T(8,128)S(1)}, u32[]{:S(2)}, u32[]{:S(2)}) collective-permute-start(f32[256,256]{1,0:T(8,128)S(1)} %get-tuple-element.13), channel_id=1, source_target_pairs={{128,0},{256,128},{384,256},{385,1},{130,2},{258,130},{386,258},{3... | collective-permute-start | bytes 786440 | tf_op jit(solution)/shard_map/ppermute | solution.py:285
  74.7 1.3 %collective-permute-start.3 = (f32[128,256]{1,0:T(8,128)S(1)}, f32[128,256]{1,0:T(8,128)S(1)}, u32[]{:S(2)}, u32[]{:S(2)}) collective-permute-start(f32[128,256]{1,0:T(8,128)S(1)} %get-tuple-element.14), channel_id=1, source_target_pairs={{256,0},{384,128},{257,1},{385,129},{258,2},{386,130},{259,3},{387... | collective-permute-start | bytes 393224 | tf_op jit(solution)/shard_map/ppermute | solution.py:286
  76.0 0.0 copy-done
  76.0 1.5 %shard_map.50.cur_ref = f32[256,256]{1,0:T(8,128)S(1)} custom-call(f32[2,4,136,128]{3,2,1,0:T(8,128)S(1)} %bitcast.9, f32[256,256]{1,0:T(8,128)S(1)} %bitcast.11), custom_call_target="tpu_custom_call" | custom-call | flops 402653184 | bytes 1081344 | tf_op jit(solution)/shard_map/pallas_call | solution.py:223
  77.5 0.9 %shard_map.51.cur_ref = f32[256,256]{1,0:T(8,128)S(1)} custom-call(f32[2,4,96,256]{3,2,1,0:T(8,128)S(1)} %bitcast.6, f32[256,256]{1,0:T(8,128)S(1)} %shard_map.50.cur_ref), custom_call_target="tpu_custom_call" | custom-call | flops 301989888 | bytes 1310720 | tf_op jit(solution)/shard_map/pallas_call | solution.py:223
  78.4 4.3 %collective-permute-done.3 = f32[128,256]{1,0:T(8,128)S(1)} collective-permute-done((f32[128,256]{1,0:T(8,128)S(1)}, f32[128,256]{1,0:T(8,128)S(1)}, u32[]{:S(2)}, u32[]{:S(2)}) %collective-permute-start.3) | collective-permute-done | bytes 131104 | tf_op jit(solution)/shard_map/ppermute | solution.py:286
  82.7 1.8 %collective-permute-done.2 = f32[256,256]{1,0:T(8,128)S(1)} collective-permute-done((f32[256,256]{1,0:T(8,128)S(1)}, f32[256,256]{1,0:T(8,128)S(1)}, u32[]{:S(2)}, u32[]{:S(2)}) %collective-permute-start.2) | collective-permute-done | bytes 262176 | tf_op jit(solution)/shard_map/ppermute | solution.py:285
  84.5 2.4 %all-gather.3 = f32[768,256]{1,0:T(8,128)S(1)} all-gather(f32[384,256]{1,0:T(8,128)S(1)} %pad_maximum_fusion), channel_id=5, replica_groups=mesh['y'=4,'zh'=4,'zl'=4,'x'=4,'core'=2] {'core'}, dimensions={0}, use_global_device_ids=true | all-gather | bytes 1179648 | tf_op jit(solution)/shard_map/all_gather | solution.py:287
  86.9 1.5 %shard_map.52 = f32[256,256]{1,0:T(8,128)} custom-call(f32[2,384,256]{2,1,0:T(8,128)S(1)} %bitcast.7, f32[256,256]{1,0:T(8,128)S(1)} %shard_map.51.cur_ref), custom_call_target="tpu_custom_call" | custom-call | flops 301989888 | bytes 1310720 | tf_op jit(solution)/shard_map/pallas_call | solution.py:223
  (5 shorter events, 0.1 us)
Async XLA Ops:
  39.4 18.6 %collective-permute-start = (f32[64,256]{1,0:T(8,128)S(1)}, f32[64,256]{1,0:T(8,128)S(1)}, u32[]{:S(2)}, u32[]{:S(2)}) collective-permute-start(f32[64,256]{1,0:T(8,128)S(1)} %get-tuple-element.10), channel_id=1, source_target_pairs={{0,96},{8,104},{16,112},{24,120},{32,0},{40,8},{48,16},{56,24},{64... | collective-permute-start | bytes 196616 | tf_op jit(solution)/shard_map/ppermute | solution.py:278
  47.2 10.8 %collective-permute-start.1 = (f32[32,256]{1,0:T(8,128)S(1)}, f32[32,256]{1,0:T(8,128)S(1)}, u32[]{:S(2)}, u32[]{:S(2)}) collective-permute-start(f32[32,256]{1,0:T(8,128)S(1)} %get-tuple-element.11), channel_id=1, source_target_pairs={{0,88},{8,80},{16,72},{24,64},{32,120},{40,112},{48,104},{56,96},{... | collective-permute-start | bytes 98312 | tf_op jit(solution)/shard_map/ppermute | solution.py:277
  72.5 3.4 %copy-start = (f32[1,256,256]{2,1,0:T(8,128)S(1)}, f32[1,256,256]{2,1,0:T(8,128)}, u32[]{:S(2)}) copy-start(f32[1,256,256]{2,1,0:T(8,128)} %param.4) | copy-start | bytes 786436
  73.4 11.1 %collective-permute-start.2 = (f32[256,256]{1,0:T(8,128)S(1)}, f32[256,256]{1,0:T(8,128)S(1)}, u32[]{:S(2)}, u32[]{:S(2)}) collective-permute-start(f32[256,256]{1,0:T(8,128)S(1)} %get-tuple-element.13), channel_id=1, source_target_pairs={{128,0},{256,128},{384,256},{385,1},{130,2},{258,130},{386,258},{3... | collective-permute-start | bytes 786440 | tf_op jit(solution)/shard_map/ppermute | solution.py:285
  74.7 8.0 %collective-permute-start.3 = (f32[128,256]{1,0:T(8,128)S(1)}, f32[128,256]{1,0:T(8,128)S(1)}, u32[]{:S(2)}, u32[]{:S(2)}) collective-permute-start(f32[128,256]{1,0:T(8,128)S(1)} %get-tuple-element.14), channel_id=1, source_target_pairs={{256,0},{384,128},{257,1},{385,129},{258,2},{386,130},{259,3},{387... | collective-permute-start | bytes 393224 | tf_op jit(solution)/shard_map/ppermute | solution.py:286

commit v2 on v1

--- a/solution.py
+++ b/solution.py
@@ -191,18 +191,18 @@
 
 def row_apply_kernel(near_ref, cur_ref, out_ref):
     row = lax.axis_index("y")
-    second = jnp.concatenate([near_ref[0, N:], near_ref[1, N:]], axis=0)
 
     @pl.when(row == 0)
     def _():
-        later = mm(split(second), split(near_ref[1, :N]))
+        third = jnp.concatenate([near_ref[0, N:], near_ref[1, N:]], axis=0)
+        later = mm(split(near_ref[1, :N]), split(third))
         first = mm(split(cur_ref[...]), split(near_ref[0, :N]))
         out_ref[...] = mm(split(first), split(later))
 
     @pl.when(row == 1)
     def _():
         first = mm(split(cur_ref[...]), split(near_ref[0, :N]))
-        out_ref[...] = mm(split(first), split(second))
+        out_ref[...] = mm(split(first), split(near_ref[1, :N]))
 
     @pl.when(row == 2)
     def _():
@@ -250,8 +250,8 @@
     ]
 
 
-ROW_ODD = from_later((1, 3))
-ROW_EVEN = [(row, row - 2) for row in range(2, 4)]
+ROW_NEAR = from_later((1, 2))
+ROW_LAST = [(3, 0)]
 
 
 def smoother(anomalies, mean_state, obs_rows, obs_precision):
@@ -282,8 +282,8 @@
     square = pltpu.VMEM(full, F32)
     total, half = call(ring_kernel, [full, (H, N)], (ring, total), 3, [square, square])
     current = call(ring_apply_kernel, full, (ring, current), 3)
-    near = lax.ppermute(total, ("y", "core"), ROW_ODD)
-    across = lax.ppermute(half, "y", ROW_EVEN)
+    near = lax.ppermute(total, ("y", "core"), ROW_NEAR)
+    across = lax.ppermute(half, "y", ROW_LAST)
     near = lax.all_gather(jnp.concatenate([near, across], axis=0), "core")
     return call(row_apply_kernel, full, (near, current), 3)[None]
 

time: 89 us -> 89.3 us (level)
  transfers between devices with their start and end apart: 4 -> 4, of which waited for: 3 -> 2; matrix products, arithmetic and copies ran while one was open for 0% -> 0% of each run, Pallas kernels for 3% -> 3%
where the time goes in v2:
time: 89.3 us; the launch traced here: 89 us
  blocking collectives  51.6 us (58%)
  starting transfers between devices  16.5 us (18%)
  waiting for transfers between devices  11.3 us (13%)
  Pallas kernels  9.29 us (10%)
    all_to_all x1, blocking collectives, smoother(): parts = lax.all_to_all(spread, 'x', 0, 0)  11.8 us
    all_to_all x1, blocking collectives, smoother(): parts = lax.all_gather(lax.all_to_all(half, 'zl', 0, 0), 'core')  9.56 us
    pallas_call x7, Pallas kernels, call(): pl.pallas_call(kernel, out_shape=shapes if many else shapes[0], in_specs=...  9.29 us
    all_to_all x1, blocking collectives, smoother(): ring = lax.all_gather(lax.all_to_all(piece, 'x', 0, 0), 'core')  8.62 us
    all_gather x1, blocking collectives, smoother(): both = lax.all_gather(gram, 'core')  8.48 us
    ppermute x1, starting transfers between devices, smoother(): near = lax.ppermute(wide, ('zh', 'zl', 'core'), NEAR)  7.8 us
    ppermute x1, waiting for transfers between devices, smoother(): across = lax.ppermute(half, 'y', ROW_LAST)  6.69 us
    ppermute x1, starting transfers between devices, smoother(): across = lax.ppermute(thin, ('zh', 'zl'), ACROSS)  6.14 us
  transfers between devices with their start and end apart: 4, of which 2 were waited for; matrix products, arithmetic and copies ran while one was open for 0% of the time, Pallas kernels for 3%

profile of v2, /device:TPU:1, one launch (start us, length us, event | category | flops | bytes accessed | tf_op | source)
XLA Modules:
  0.0 89.0 jit_solution(9072638179036763684)
XLA Ops:
  0.0 1.8 %shard_map.46 = f32[272,128]{1,0:T(8,128)S(1)} custom-call(f32[256,256]{1,0:T(8,128)} %bitcast.10, f32[1,256]{1,0:T(1,128)} %refs_1_.1, s32[1,128]{1,0:T(1,128)} %refs_2_.1, f32[1,128]{1,0:T(1,128)} %refs_3_.1), custom_call_target="tpu_custom_call" | custom-call | flops 100663296 | bytes 403456 | tf_op jit(solution)/shard_map/pallas_call | solution.py:223
  1.8 8.5 %all-gather = f32[544,128]{1,0:T(8,128)S(1)} all-gather(f32[272,128]{1,0:T(8,128)S(1)} %shard_map.46), channel_id=2, replica_groups=mesh['y'=4,'zh'=4,'zl'=4,'x'=4,'core'=2] {'core'}, dimensions={0}, use_global_device_ids=true | all-gather | bytes 417792 | tf_op jit(solution)/shard_map/all_gather | solution.py:268
  10.3 11.8 %all_to_all.15.parts_ref = f32[4,272,128]{2,1,0:T(8,128)S(1)} all-to-all(f32[4,272,128]{2,1,0:T(8,128)S(1)} %broadcast_in_dim.9), channel_id=1, replica_groups=mesh['y'=4,'zh'=4,'zl'=4,'x'=4,'core'=2] {'x'}, dimensions={0} | all-to-all | bytes 1114112 | tf_op jit(solution)/shard_map/all_to_all | solution.py:270
  22.2 1.9 %shard_map.47 = f32[4,136,128]{2,1,0:T(8,128)S(1)} custom-call(f32[4,272,128]{2,1,0:T(8,128)S(1)} %all_to_all.15.parts_ref), custom_call_target="tpu_custom_call" | custom-call | flops 603979776 | bytes 835584 | tf_op jit(solution)/shard_map/pallas_call | solution.py:223
  24.1 9.6 %all_to_all.16 = f32[4,136,128]{2,1,0:T(8,128)S(1)} all-to-all(f32[4,136,128]{2,1,0:T(8,128)S(1)} %shard_map.47), channel_id=1, replica_groups=mesh['y'=4,'zh'=4,'zl'=4,'x'=4,'core'=2] {'zl'}, dimensions={0} | all-to-all | bytes 557056 | tf_op jit(solution)/shard_map/all_to_all | solution.py:272
  33.7 4.8 %all-gather.1 = f32[8,136,128]{2,1,0:T(8,128)S(1)} all-gather(f32[4,136,128]{2,1,0:T(8,128)S(1)} %all_to_all.16), channel_id=3, replica_groups=mesh['y'=4,'zh'=4,'zl'=4,'x'=4,'core'=2] {'core'}, dimensions={0}, use_global_device_ids=true | all-gather | bytes 835584 | tf_op jit(solution)/shard_map/all_gather | solution.py:272
  38.5 0.9 %shard_map.48 = (f32[256,256]{1,0:T(8,128)S(1)}, f32[64,256]{1,0:T(8,128)S(1)}, f32[32,256]{1,0:T(8,128)S(1)}) custom-call(f32[2,4,136,128]{3,2,1,0:T(8,128)S(1)} %bitcast.8), custom_call_target="tpu_custom_call" | custom-call | flops 301989888 | bytes 917504 | tf_op jit(solution)/shard_map/pallas_call | solution.py:223
  39.4 7.8 %collective-permute-start = (f32[64,256]{1,0:T(8,128)S(1)}, f32[64,256]{1,0:T(8,128)S(1)}, u32[]{:S(2)}, u32[]{:S(2)}) collective-permute-start(f32[64,256]{1,0:T(8,128)S(1)} %get-tuple-element.10), channel_id=1, source_target_pairs={{0,96},{8,104},{16,112},{24,120},{32,0},{40,8},{48,16},{56,24},{64... | collective-permute-start | bytes 196616 | tf_op jit(solution)/shard_map/ppermute | solution.py:278
  47.2 6.1 %collective-permute-start.1 = (f32[32,256]{1,0:T(8,128)S(1)}, f32[32,256]{1,0:T(8,128)S(1)}, u32[]{:S(2)}, u32[]{:S(2)}) collective-permute-start(f32[32,256]{1,0:T(8,128)S(1)} %get-tuple-element.11), channel_id=1, source_target_pairs={{0,88},{8,80},{16,72},{24,64},{32,120},{40,112},{48,104},{56,96},{... | collective-permute-start | bytes 98312 | tf_op jit(solution)/shard_map/ppermute | solution.py:277
  53.3 4.6 %collective-permute-done.1 = f32[32,256]{1,0:T(8,128)S(1)} collective-permute-done((f32[32,256]{1,0:T(8,128)S(1)}, f32[32,256]{1,0:T(8,128)S(1)}, u32[]{:S(2)}, u32[]{:S(2)}) %collective-permute-start.1) | collective-permute-done | bytes 32800 | tf_op jit(solution)/shard_map/ppermute | solution.py:277
  58.0 0.0 collective-permute-done
  58.0 8.6 %all_to_all.17 = f32[4,96,256]{2,1,0:T(8,128)S(1)} all-to-all(f32[4,96,256]{2,1,0:T(8,128)S(1)} %broadcast_in_dim.10), channel_id=1, replica_groups=mesh['y'=4,'zh'=4,'zl'=4,'x'=4,'core'=2] {'x'}, dimensions={0} | all-to-all | bytes 786432 | tf_op jit(solution)/shard_map/all_to_all | solution.py:281
  66.6 5.9 %all-gather.2 = f32[8,96,256]{2,1,0:T(8,128)S(1)} all-gather(f32[4,96,256]{2,1,0:T(8,128)S(1)} %all_to_all.17), channel_id=4, replica_groups=mesh['y'=4,'zh'=4,'zl'=4,'x'=4,'core'=2] {'core'}, dimensions={0}, use_global_device_ids=true | all-gather | bytes 1179648 | tf_op jit(solution)/shard_map/all_gather | solution.py:281
  72.5 0.0 copy-start
  72.5 0.8 shard_map.49
  73.4 1.3 %collective-permute-start.2 = (f32[256,256]{1,0:T(8,128)S(1)}, f32[256,256]{1,0:T(8,128)S(1)}, u32[]{:S(2)}, u32[]{:S(2)}) collective-permute-start(f32[256,256]{1,0:T(8,128)S(1)} %get-tuple-element.13), channel_id=1, source_target_pairs={{128,0},{256,128},{384,256},{257,1},{385,129},{130,2},{258,130},{3... | collective-permute-start | bytes 786440 | tf_op jit(solution)/shard_map/ppermute | solution.py:285
  74.7 1.3 %collective-permute-start.3 = (f32[128,256]{1,0:T(8,128)S(1)}, f32[128,256]{1,0:T(8,128)S(1)}, u32[]{:S(2)}, u32[]{:S(2)}) collective-permute-start(f32[128,256]{1,0:T(8,128)S(1)} %get-tuple-element.14), channel_id=1, source_target_pairs={{384,0},{385,1},{386,2},{387,3},{388,4},{389,5},{390,6},{391,7},{3... | collective-permute-start | bytes 393224 | tf_op jit(solution)/shard_map/ppermute | solution.py:286
  76.0 0.0 copy-done
  76.0 1.5 %shard_map.50.cur_ref = f32[256,256]{1,0:T(8,128)S(1)} custom-call(f32[2,4,136,128]{3,2,1,0:T(8,128)S(1)} %bitcast.9, f32[256,256]{1,0:T(8,128)S(1)} %bitcast.11), custom_call_target="tpu_custom_call" | custom-call | flops 402653184 | bytes 1081344 | tf_op jit(solution)/shard_map/pallas_call | solution.py:223
  77.5 0.9 %shard_map.51.cur_ref = f32[256,256]{1,0:T(8,128)S(1)} custom-call(f32[2,4,96,256]{3,2,1,0:T(8,128)S(1)} %bitcast.6, f32[256,256]{1,0:T(8,128)S(1)} %shard_map.50.cur_ref), custom_call_target="tpu_custom_call" | custom-call | flops 301989888 | bytes 1310720 | tf_op jit(solution)/shard_map/pallas_call | solution.py:223
  78.4 6.7 %collective-permute-done.3 = f32[128,256]{1,0:T(8,128)S(1)} collective-permute-done((f32[128,256]{1,0:T(8,128)S(1)}, f32[128,256]{1,0:T(8,128)S(1)}, u32[]{:S(2)}, u32[]{:S(2)}) %collective-permute-start.3) | collective-permute-done | bytes 131104 | tf_op jit(solution)/shard_map/ppermute | solution.py:286
  85.1 0.0 collective-permute-done.2
  85.1 2.4 %all-gather.3 = f32[768,256]{1,0:T(8,128)S(1)} all-gather(f32[384,256]{1,0:T(8,128)S(1)} %pad_maximum_fusion), channel_id=5, replica_groups=mesh['y'=4,'zh'=4,'zl'=4,'x'=4,'core'=2] {'core'}, dimensions={0}, use_global_device_ids=true | all-gather | bytes 1179648 | tf_op jit(solution)/shard_map/all_gather | solution.py:287
  87.5 1.4 %shard_map.52 = f32[256,256]{1,0:T(8,128)} custom-call(f32[2,384,256]{2,1,0:T(8,128)S(1)} %bitcast.7, f32[256,256]{1,0:T(8,128)S(1)} %shard_map.51.cur_ref), custom_call_target="tpu_custom_call" | custom-call | flops 301989888 | bytes 1310720 | tf_op jit(solution)/shard_map/pallas_call | solution.py:223
  (5 shorter events, 0.1 us)
Async XLA Ops:
  39.4 18.6 %collective-permute-start = (f32[64,256]{1,0:T(8,128)S(1)}, f32[64,256]{1,0:T(8,128)S(1)}, u32[]{:S(2)}, u32[]{:S(2)}) collective-permute-start(f32[64,256]{1,0:T(8,128)S(1)} %get-tuple-element.10), channel_id=1, source_target_pairs={{0,96},{8,104},{16,112},{24,120},{32,0},{40,8},{48,16},{56,24},{64... | collective-permute-start | bytes 196616 | tf_op jit(solution)/shard_map/ppermute | solution.py:278
  47.2 10.8 %collective-permute-start.1 = (f32[32,256]{1,0:T(8,128)S(1)}, f32[32,256]{1,0:T(8,128)S(1)}, u32[]{:S(2)}, u32[]{:S(2)}) collective-permute-start(f32[32,256]{1,0:T(8,128)S(1)} %get-tuple-element.11), channel_id=1, source_target_pairs={{0,88},{8,80},{16,72},{24,64},{32,120},{40,112},{48,104},{56,96},{... | collective-permute-start | bytes 98312 | tf_op jit(solution)/shard_map/ppermute | solution.py:277
  72.5 3.4 %copy-start = (f32[1,256,256]{2,1,0:T(8,128)S(1)}, f32[1,256,256]{2,1,0:T(8,128)}, u32[]{:S(2)}) copy-start(f32[1,256,256]{2,1,0:T(8,128)} %param.4) | copy-start | bytes 786436
  73.4 11.7 %collective-permute-start.2 = (f32[256,256]{1,0:T(8,128)S(1)}, f32[256,256]{1,0:T(8,128)S(1)}, u32[]{:S(2)}, u32[]{:S(2)}) collective-permute-start(f32[256,256]{1,0:T(8,128)S(1)} %get-tuple-element.13), channel_id=1, source_target_pairs={{128,0},{256,128},{384,256},{257,1},{385,129},{130,2},{258,130},{3... | collective-permute-start | bytes 786440 | tf_op jit(solution)/shard_map/ppermute | solution.py:285
  74.7 10.4 %collective-permute-start.3 = (f32[128,256]{1,0:T(8,128)S(1)}, f32[128,256]{1,0:T(8,128)S(1)}, u32[]{:S(2)}, u32[]{:S(2)}) collective-permute-start(f32[128,256]{1,0:T(8,128)S(1)} %get-tuple-element.14), channel_id=1, source_target_pairs={{384,0},{385,1},{386,2},{387,3},{388,4},{389,5},{390,6},{391,7},{3... | collective-permute-start | bytes 393224 | tf_op jit(solution)/shard_map/ppermute | solution.py:286

commit v3 on v2

--- a/solution.py
+++ b/solution.py
@@ -14,7 +14,7 @@
 H = 128
 PACK = 272
 NS_STEPS = 3
-WIDE, THIN = N // 4, N // 8
+THIN = N // 8
 VMEM_BYTES = 8 * 1024 * 1024
 
 
@@ -121,17 +121,21 @@
     return out
 
 
-def slices(total_ref, wide_ref, thin_ref):
-    chip = lax.axis_index("x")
-    core = lax.axis_index("core")
-    wide_ref[...] = total_ref[pl.ds(pl.multiple_of(chip * WIDE, 8), WIDE), :]
-    thin_ref[...] = total_ref[pl.ds(pl.multiple_of(core * H + chip * THIN, 8), THIN), :]
-
-
-def quad_kernel(parts_ref, total_ref, wide_ref, thin_ref):
+def quad_kernel(parts_ref, total_ref, slice_ref):
     one, two, three, four = [split(t) for t in transforms(parts_ref)]
     total_ref[...] = mm(split(mm(one, two)), split(mm(three, four)))
-    slices(total_ref, wide_ref, thin_ref)
+    place = 2 * lax.axis_index("x") + lax.axis_index("core")
+    rows = total_ref[pl.ds(pl.multiple_of(place * THIN, 8), THIN), :]
+    for copy in range(4):
+        slice_ref[copy] = rows
+
+
+def pick_kernel(slices_ref, out_ref):
+    quad = lax.axis_index("zh")
+    for place in range(3):
+        rows = slices_ref[lax.rem(quad + place + 1, 4)]
+        for copy in range(4):
+            out_ref[copy, place * THIN : (place + 1) * THIN, :] = rows
 
 
 def quad_apply_kernel(parts_ref, cur_ref, out_ref):
@@ -146,10 +150,12 @@
 
 
 def joined(ring_ref):
-    after = ring_ref[0, :, :WIDE].reshape(N, N)
-    before = ring_ref[1, :, :WIDE].reshape(N, N)
-    across = [ring_ref[core, :, WIDE:].reshape(H, N) for core in range(2)]
-    return after, jnp.concatenate(across, axis=0), before
+    out = []
+    for place in range(3):
+        rows = slice(place * THIN, (place + 1) * THIN)
+        pieces = [ring_ref[core, chip, rows] for chip in range(4) for core in range(2)]
+        out.append(jnp.concatenate(pieces, axis=0))
+    return out
 
 
 def ring_kernel(ring_ref, mine_ref, total_ref, half_ref, one, two):
@@ -231,15 +237,6 @@
             flops=products * 6 * N * N * N, bytes_accessed=moved, transcendentals=0
         ),
     )(*args)
-
-
-RING = 16
-NEAR = [
-    (2 * z + core, 2 * ((z + step) % RING) + core)
-    for core, step in enumerate((-4, 4))
-    for z in range(RING)
-]
-ACROSS = [(z, (11 - z) if z % 8 < 4 else (19 - z)) for z in range(RING)]
 
 
 def from_later(steps):
@@ -271,13 +268,10 @@
     half = call(root_kernel, (4, PACK // 2, H), (parts,), 6, [pltpu.VMEM((PACK, H), F32)])
     parts = lax.all_gather(lax.all_to_all(half, "zl", 0, 0), "core")
     full = (N, N)
-    wide, thin = (WIDE, N), (THIN, N)
-    total, wide, thin = call(quad_kernel, [full, wide, thin], (parts,), 3)
+    total, piece = call(quad_kernel, [full, (4, THIN, N)], (parts,), 3)
     current = call(quad_apply_kernel, full, (parts, current), 4)
-    across = lax.ppermute(thin, ("zh", "zl"), ACROSS)
-    near = lax.ppermute(wide, ("zh", "zl", "core"), NEAR)
-    piece = jnp.concatenate([near, across], axis=0)
-    piece = jnp.broadcast_to(piece, (4, WIDE + THIN, N))
+    piece = lax.all_to_all(piece, "zh", 0, 0)
+    piece = call(pick_kernel, (4, 3 * THIN, N), (piece,), 0)
     ring = lax.all_gather(lax.all_to_all(piece, "x", 0, 0), "core")
     square = pltpu.VMEM(full, F32)
     total, half = call(ring_kernel, [full, (H, N)], (ring, total), 3, [square, square])

time: 89.3 us -> 94.8 us (1.062)
  blocking collectives: 51.6 us -> 75.7 us
  starting transfers between devices: 16.5 us -> 2.58 us
  waiting for transfers between devices: 11.3 us -> 6.69 us
    all_to_all x0 -> x1, blocking collectives: none -> 23 us  [smoother(): piece = lax.all_to_all(piece, 'zh', 0, 0)]
    ppermute x2 -> x0, starting transfers between devices: 13.9 us -> none  [the longest x1 7.8 us: smoother(): near = lax.ppermute(wide, ('zh', 'zl', 'core'), NEAR)]
    ppermute x2 -> x0, waiting for transfers between devices: 4.63 us -> none  [the longest x1 4.63 us: smoother(): across = lax.ppermute(thin, ('zh', 'zl'), ACROSS)]
    all_gather x1, blocking collectives: 5.89 us -> 7.07 us  [smoother(): ring = lax.all_gather(lax.all_to_all(piece, 'x', 0, 0), 'core')]
    pallas_call x7 -> x8, Pallas kernels: 9.29 us -> 9.31 us  [call(): pl.pallas_call(kernel, out_shape=shapes if many else shapes[0], in_specs=...]
  transfers between devices with their start and end apart: 4 -> 2, of which waited for: 2 -> 1; matrix products, arithmetic and copies ran while one was open for 0% -> 0% of each run, Pallas kernels for 3% -> 3%
where the time goes in v3:
time: 94.8 us; the launch traced here: 94.5 us
  blocking collectives  75.7 us (80%)
  Pallas kernels  9.31 us (10%)
  waiting for transfers between devices  6.69 us (7%)
  starting transfers between devices  2.58 us (3%)
    all_to_all x1, blocking collectives, smoother(): piece = lax.all_to_all(piece, 'zh', 0, 0)  23 us
    all_to_all x1, blocking collectives, smoother(): parts = lax.all_to_all(spread, 'x', 0, 0)  11.8 us
    all_to_all x1, blocking collectives, smoother(): parts = lax.all_gather(lax.all_to_all(half, 'zl', 0, 0), 'core')  9.56 us
    pallas_call x8, Pallas kernels, call(): pl.pallas_call(kernel, out_shape=shapes if many else shapes[0], in_specs=...  9.31 us
    all_to_all x1, blocking collectives, smoother(): ring = lax.all_gather(lax.all_to_all(piece, 'x', 0, 0), 'core')  8.62 us
    all_gather x1, blocking collectives, smoother(): both = lax.all_gather(gram, 'core')  8.48 us
    all_gather x1, blocking collectives, smoother(): ring = lax.all_gather(lax.all_to_all(piece, 'x', 0, 0), 'core')  7.07 us
    ppermute x1, waiting for transfers between devices, smoother(): across = lax.ppermute(half, 'y', ROW_LAST)  6.69 us
  transfers between devices with their start and end apart: 2, of which 1 were waited for; matrix products, arithmetic and copies ran while one was open for 0% of the time, Pallas kernels for 3%

profile of v3, /device:TPU:1, one launch (start us, length us, event | category | flops | bytes accessed | tf_op | source)
XLA Modules:
  0.0 94.5 jit_solution(13505043317468597546)
XLA Ops:
  0.0 1.8 %shard_map.46 = f32[272,128]{1,0:T(8,128)S(1)} custom-call(f32[256,256]{1,0:T(8,128)} %bitcast.10, f32[1,256]{1,0:T(1,128)} %refs_1_.1, s32[1,128]{1,0:T(1,128)} %refs_2_.1, f32[1,128]{1,0:T(1,128)} %refs_3_.1), custom_call_target="tpu_custom_call" | custom-call | flops 100663296 | bytes 403456 | tf_op jit(solution)/shard_map/pallas_call | solution.py:229
  1.8 8.5 %all-gather = f32[544,128]{1,0:T(8,128)S(1)} all-gather(f32[272,128]{1,0:T(8,128)S(1)} %shard_map.46), channel_id=2, replica_groups=mesh['y'=4,'zh'=4,'zl'=4,'x'=4,'core'=2] {'core'}, dimensions={0}, use_global_device_ids=true | all-gather | bytes 417792 | tf_op jit(solution)/shard_map/all_gather | solution.py:265
  10.3 11.8 %all_to_all.20.parts_ref = f32[4,272,128]{2,1,0:T(8,128)S(1)} all-to-all(f32[4,272,128]{2,1,0:T(8,128)S(1)} %broadcast_in_dim.6), channel_id=1, replica_groups=mesh['y'=4,'zh'=4,'zl'=4,'x'=4,'core'=2] {'x'}, dimensions={0} | all-to-all | bytes 1114112 | tf_op jit(solution)/shard_map/all_to_all | solution.py:267
  22.2 1.9 %shard_map.47 = f32[4,136,128]{2,1,0:T(8,128)S(1)} custom-call(f32[4,272,128]{2,1,0:T(8,128)S(1)} %all_to_all.20.parts_ref), custom_call_target="tpu_custom_call" | custom-call | flops 603979776 | bytes 835584 | tf_op jit(solution)/shard_map/pallas_call | solution.py:229
  24.1 9.6 %all_to_all.21 = f32[4,136,128]{2,1,0:T(8,128)S(1)} all-to-all(f32[4,136,128]{2,1,0:T(8,128)S(1)} %shard_map.47), channel_id=1, replica_groups=mesh['y'=4,'zh'=4,'zl'=4,'x'=4,'core'=2] {'zl'}, dimensions={0} | all-to-all | bytes 557056 | tf_op jit(solution)/shard_map/all_to_all | solution.py:269
  33.7 4.8 %all-gather.1 = f32[8,136,128]{2,1,0:T(8,128)S(1)} all-gather(f32[4,136,128]{2,1,0:T(8,128)S(1)} %all_to_all.21), channel_id=3, replica_groups=mesh['y'=4,'zh'=4,'zl'=4,'x'=4,'core'=2] {'core'}, dimensions={0}, use_global_device_ids=true | all-gather | bytes 835584 | tf_op jit(solution)/shard_map/all_gather | solution.py:269
  38.5 0.9 shard_map.48
  39.4 23.0 %all_to_all.22.slices_ref = f32[4,32,256]{2,1,0:T(8,128)S(1)} all-to-all(f32[4,32,256]{2,1,0:T(8,128)S(1)} %get-tuple-element.9), channel_id=1, replica_groups=mesh['y'=4,'zh'=4,'zl'=4,'x'=4,'core'=2] {'zh'}, dimensions={0} | all-to-all | bytes 262144 | tf_op jit(solution)/shard_map/all_to_all | solution.py:273
  62.4 8.6 %all_to_all.23 = f32[4,96,256]{2,1,0:T(8,128)S(1)} all-to-all(f32[4,96,256]{2,1,0:T(8,128)S(1)} %shard_map.49), channel_id=1, replica_groups=mesh['y'=4,'zh'=4,'zl'=4,'x'=4,'core'=2] {'x'}, dimensions={0} | all-to-all | bytes 786432 | tf_op jit(solution)/shard_map/all_to_all | solution.py:275
  71.0 7.1 %all-gather.2 = f32[8,96,256]{2,1,0:T(8,128)S(1)} all-gather(f32[4,96,256]{2,1,0:T(8,128)S(1)} %all_to_all.23), channel_id=4, replica_groups=mesh['y'=4,'zh'=4,'zl'=4,'x'=4,'core'=2] {'core'}, dimensions={0}, use_global_device_ids=true | all-gather | bytes 1179648 | tf_op jit(solution)/shard_map/all_gather | solution.py:275
  78.1 0.0 copy-start
  78.1 0.8 shard_map.50
  78.9 1.3 %collective-permute-start = (f32[256,256]{1,0:T(8,128)S(1)}, f32[256,256]{1,0:T(8,128)S(1)}, u32[]{:S(2)}, u32[]{:S(2)}) collective-permute-start(f32[256,256]{1,0:T(8,128)S(1)} %get-tuple-element.11), channel_id=1, source_target_pairs={{128,0},{256,128},{384,256},{257,1},{385,129},{130,2},{258,130},{3... | collective-permute-start | bytes 786440 | tf_op jit(solution)/shard_map/ppermute | solution.py:279
  80.2 1.3 %collective-permute-start.1 = (f32[128,256]{1,0:T(8,128)S(1)}, f32[128,256]{1,0:T(8,128)S(1)}, u32[]{:S(2)}, u32[]{:S(2)}) collective-permute-start(f32[128,256]{1,0:T(8,128)S(1)} %get-tuple-element.12), channel_id=1, source_target_pairs={{384,0},{385,1},{386,2},{387,3},{388,4},{389,5},{390,6},{391,7},{3... | collective-permute-start | bytes 393224 | tf_op jit(solution)/shard_map/ppermute | solution.py:280
  81.5 0.0 copy-done
  81.5 1.5 %shard_map.51.cur_ref = f32[256,256]{1,0:T(8,128)S(1)} custom-call(f32[2,4,136,128]{3,2,1,0:T(8,128)S(1)} %bitcast.9, f32[256,256]{1,0:T(8,128)S(1)} %bitcast.11), custom_call_target="tpu_custom_call" | custom-call | flops 402653184 | bytes 1081344 | tf_op jit(solution)/shard_map/pallas_call | solution.py:229
  83.0 0.9 shard_map.52.cur_ref
  83.9 6.7 %collective-permute-done.1 = f32[128,256]{1,0:T(8,128)S(1)} collective-permute-done((f32[128,256]{1,0:T(8,128)S(1)}, f32[128,256]{1,0:T(8,128)S(1)}, u32[]{:S(2)}, u32[]{:S(2)}) %collective-permute-start.1) | collective-permute-done | bytes 131104 | tf_op jit(solution)/shard_map/ppermute | solution.py:280
  90.6 0.0 collective-permute-done
  90.6 2.4 %all-gather.3 = f32[768,256]{1,0:T(8,128)S(1)} all-gather(f32[384,256]{1,0:T(8,128)S(1)} %pad_maximum_fusion), channel_id=5, replica_groups=mesh['y'=4,'zh'=4,'zl'=4,'x'=4,'core'=2] {'core'}, dimensions={0}, use_global_device_ids=true | all-gather | bytes 1179648 | tf_op jit(solution)/shard_map/all_gather | solution.py:281
  93.0 1.4 %shard_map.53 = f32[256,256]{1,0:T(8,128)} custom-call(f32[2,384,256]{2,1,0:T(8,128)S(1)} %bitcast.7, f32[256,256]{1,0:T(8,128)S(1)} %shard_map.52.cur_ref), custom_call_target="tpu_custom_call" | custom-call | flops 301989888 | bytes 1310720 | tf_op jit(solution)/shard_map/pallas_call | solution.py:229
  (4 shorter events, 0.1 us)
Async XLA Ops:
  78.1 3.4 %copy-start = (f32[1,256,256]{2,1,0:T(8,128)S(1)}, f32[1,256,256]{2,1,0:T(8,128)}, u32[]{:S(2)}) copy-start(f32[1,256,256]{2,1,0:T(8,128)} %param.4) | copy-start | bytes 786436
  78.9 11.7 %collective-permute-start = (f32[256,256]{1,0:T(8,128)S(1)}, f32[256,256]{1,0:T(8,128)S(1)}, u32[]{:S(2)}, u32[]{:S(2)}) collective-permute-start(f32[256,256]{1,0:T(8,128)S(1)} %get-tuple-element.11), channel_id=1, source_target_pairs={{128,0},{256,128},{384,256},{257,1},{385,129},{130,2},{258,130},{3... | collective-permute-start | bytes 786440 | tf_op jit(solution)/shard_map/ppermute | solution.py:279
  80.2 10.4 %collective-permute-start.1 = (f32[128,256]{1,0:T(8,128)S(1)}, f32[128,256]{1,0:T(8,128)S(1)}, u32[]{:S(2)}, u32[]{:S(2)}) collective-permute-start(f32[128,256]{1,0:T(8,128)S(1)} %get-tuple-element.12), channel_id=1, source_target_pairs={{384,0},{385,1},{386,2},{387,3},{388,4},{389,5},{390,6},{391,7},{3... | collective-permute-start | bytes 393224 | tf_op jit(solution)/shard_map/ppermute | solution.py:280

commit v4 on v1

--- a/solution.py
+++ b/solution.py
@@ -89,8 +89,15 @@
     pack(gram, out_ref)
 
 
-def root_kernel(parts_ref, out_ref, packed):
-    total = (parts_ref[0] + parts_ref[1]) + (parts_ref[2] + parts_ref[3])
+def halve_kernel(both_ref, out_ref):
+    rows = pl.ds(pl.multiple_of(lax.axis_index("core") * (PACK // 2), 8), PACK // 2)
+    total = both_ref[0, rows, :] + both_ref[1, rows, :]
+    for copy in range(4):
+        out_ref[copy] = total
+
+
+def root_kernel(halves_ref, out_ref, packed):
+    total = jnp.concatenate([halves_ref[0], halves_ref[1]], axis=0)
     i, j = eye_mask(N)
     unit = jnp.where(i == j, 1.0, 0.0)
     system = unpack(total) + unit
@@ -266,16 +273,17 @@
         pl.BlockSpec(memory_space=pltpu.HBM),
     )
     both = lax.all_gather(gram, "core")
-    spread = jnp.broadcast_to(both[0] + both[1], (4, PACK, H))
+    spread = call(halve_kernel, (4, PACK // 2, H), (both,), 0)
     parts = lax.all_to_all(spread, "x", 0, 0)
+    parts = lax.all_gather((parts[0] + parts[1]) + (parts[2] + parts[3]), "core")
     half = call(root_kernel, (4, PACK // 2, H), (parts,), 6, [pltpu.VMEM((PACK, H), F32)])
     parts = lax.all_gather(lax.all_to_all(half, "zl", 0, 0), "core")
     full = (N, N)
     wide, thin = (WIDE, N), (THIN, N)
     total, wide, thin = call(quad_kernel, [full, wide, thin], (parts,), 3)
     current = call(quad_apply_kernel, full, (parts, current), 4)
+    near = lax.ppermute(wide, ("zh", "zl", "core"), NEAR)
     across = lax.ppermute(thin, ("zh", "zl"), ACROSS)
-    near = lax.ppermute(wide, ("zh", "zl", "core"), NEAR)
     piece = jnp.concatenate([near, across], axis=0)
     piece = jnp.broadcast_to(piece, (4, WIDE + THIN, N))
     ring = lax.all_gather(lax.all_to_all(piece, "x", 0, 0), "core")

time: 89 us -> 89.1 us (level)
    all_to_all x1, blocking collectives: 11.8 us -> 8.93 us  [smoother(): parts = lax.all_to_all(spread, 'x', 0, 0)]
    all_gather x0 -> x1, blocking collectives: none -> 2.78 us  [smoother(): parts = lax.all_gather(parts[0] + parts[1] + (parts[2] + parts[3]), 'core')]
    all_to_all x1, blocking collectives: 9.56 us -> 10.9 us  [smoother(): parts = lax.all_gather(lax.all_to_all(half, 'zl', 0, 0), 'core')]
    all_gather x1, blocking collectives: 4.8 us -> 3.47 us  [smoother(): parts = lax.all_gather(lax.all_to_all(half, 'zl', 0, 0), 'core')]
    pallas_call x7 -> x8, Pallas kernels: 9.31 us -> 9.33 us  [call(): pl.pallas_call(kernel, out_shape=shapes if many else shapes[0], in_specs=...]
where the time goes in v4:
time: 89.1 us; the launch traced here: 88.4 us
  blocking collectives  51.4 us (58%)
  starting transfers between devices  16.7 us (19%)
  waiting for transfers between devices  10.8 us (12%)
  Pallas kernels  9.33 us (10%)
    all_to_all x1, blocking collectives, smoother(): parts = lax.all_gather(lax.all_to_all(half, 'zl', 0, 0), 'core')  10.9 us
    pallas_call x8, Pallas kernels, call(): pl.pallas_call(kernel, out_shape=shapes if many else shapes[0], in_specs=...  9.33 us
    all_to_all x1, blocking collectives, smoother(): parts = lax.all_to_all(spread, 'x', 0, 0)  8.93 us
    all_to_all x1, blocking collectives, smoother(): ring = lax.all_gather(lax.all_to_all(piece, 'x', 0, 0), 'core')  8.62 us
    all_gather x1, blocking collectives, smoother(): both = lax.all_gather(gram, 'core')  8.48 us
    ppermute x1, starting transfers between devices, smoother(): near = lax.ppermute(wide, ('zh', 'zl', 'core'), NEAR)  7.99 us
    ppermute x1, starting transfers between devices, smoother(): across = lax.ppermute(thin, ('zh', 'zl'), ACROSS)  6.14 us
    all_gather x1, blocking collectives, smoother(): ring = lax.all_gather(lax.all_to_all(piece, 'x', 0, 0), 'core')  5.88 us
  transfers between devices with their start and end apart: 4, of which 3 were waited for; matrix products, arithmetic and copies ran while one was open for 0% of the time, Pallas kernels for 3%

profile of v4, /device:TPU:1, one launch (start us, length us, event | category | flops | bytes accessed | tf_op | source)
XLA Modules:
  0.0 88.4 jit_solution(7041097204421155962)
XLA Ops:
  0.0 1.8 %shard_map.46 = f32[272,128]{1,0:T(8,128)S(1)} custom-call(f32[256,256]{1,0:T(8,128)} %bitcast.12, f32[1,256]{1,0:T(1,128)} %refs_1_.1, s32[1,128]{1,0:T(1,128)} %refs_2_.1, f32[1,128]{1,0:T(1,128)} %refs_3_.1), custom_call_target="tpu_custom_call" | custom-call | flops 100663296 | bytes 403456 | tf_op jit(solution)/shard_map/pallas_call | solution.py:230
  1.8 8.5 %all-gather = f32[544,128]{1,0:T(8,128)S(1)} all-gather(f32[272,128]{1,0:T(8,128)S(1)} %shard_map.46), channel_id=2, replica_groups=mesh['y'=4,'zh'=4,'zl'=4,'x'=4,'core'=2] {'core'}, dimensions={0}, use_global_device_ids=true | all-gather | bytes 417792 | tf_op jit(solution)/shard_map/all_gather | solution.py:275
  10.3 8.9 %all_to_all.15 = f32[4,136,128]{2,1,0:T(8,128)S(1)} all-to-all(f32[4,136,128]{2,1,0:T(8,128)S(1)} %shard_map.47), channel_id=1, replica_groups=mesh['y'=4,'zh'=4,'zl'=4,'x'=4,'core'=2] {'x'}, dimensions={0} | all-to-all | bytes 557056 | tf_op jit(solution)/shard_map/all_to_all | solution.py:277
  19.2 2.8 %all_gather.30.halves_ref = f32[2,136,128]{2,1,0:T(8,128)S(1)} all-gather(f32[1,136,128]{2,1,0:T(8,128)S(1)} %fusion), channel_id=1, replica_groups=mesh['y'=4,'zh'=4,'zl'=4,'x'=4,'core'=2] {'core'}, dimensions={0}, use_global_device_ids=true | all-gather | bytes 208896 | tf_op jit(solution)/shard_map/all_gather | solution.py:278
  22.0 1.9 %shard_map.48 = f32[4,136,128]{2,1,0:T(8,128)S(1)} custom-call(f32[2,136,128]{2,1,0:T(8,128)S(1)} %all_gather.30.halves_ref), custom_call_target="tpu_custom_call" | custom-call | flops 603979776 | bytes 417792 | tf_op jit(solution)/shard_map/pallas_call | solution.py:230
  24.0 10.9 %all_to_all.16 = f32[4,136,128]{2,1,0:T(8,128)S(1)} all-to-all(f32[4,136,128]{2,1,0:T(8,128)S(1)} %shard_map.48), channel_id=1, replica_groups=mesh['y'=4,'zh'=4,'zl'=4,'x'=4,'core'=2] {'zl'}, dimensions={0} | all-to-all | bytes 557056 | tf_op jit(solution)/shard_map/all_to_all | solution.py:280
  34.9 3.5 %all-gather.1 = f32[8,136,128]{2,1,0:T(8,128)S(1)} all-gather(f32[4,136,128]{2,1,0:T(8,128)S(1)} %all_to_all.16), channel_id=3, replica_groups=mesh['y'=4,'zh'=4,'zl'=4,'x'=4,'core'=2] {'core'}, dimensions={0}, use_global_device_ids=true | all-gather | bytes 835584 | tf_op jit(solution)/shard_map/all_gather | solution.py:280
  38.3 0.9 %shard_map.49 = (f32[256,256]{1,0:T(8,128)S(1)}, f32[64,256]{1,0:T(8,128)S(1)}, f32[32,256]{1,0:T(8,128)S(1)}) custom-call(f32[2,4,136,128]{3,2,1,0:T(8,128)S(1)} %bitcast.10), custom_call_target="tpu_custom_call" | custom-call | flops 301989888 | bytes 917504 | tf_op jit(solution)/shard_map/pallas_call | solution.py:230
  39.2 8.0 %collective-permute-start = (f32[64,256]{1,0:T(8,128)S(1)}, f32[64,256]{1,0:T(8,128)S(1)}, u32[]{:S(2)}, u32[]{:S(2)}) collective-permute-start(f32[64,256]{1,0:T(8,128)S(1)} %get-tuple-element.10), channel_id=1, source_target_pairs={{0,96},{8,104},{16,112},{24,120},{32,0},{40,8},{48,16},{56,24},{64... | collective-permute-start | bytes 196616 | tf_op jit(solution)/shard_map/ppermute | solution.py:285
  47.2 6.1 %collective-permute-start.1 = (f32[32,256]{1,0:T(8,128)S(1)}, f32[32,256]{1,0:T(8,128)S(1)}, u32[]{:S(2)}, u32[]{:S(2)}) collective-permute-start(f32[32,256]{1,0:T(8,128)S(1)} %get-tuple-element.11), channel_id=1, source_target_pairs={{0,88},{8,80},{16,72},{24,64},{32,120},{40,112},{48,104},{56,96},{... | collective-permute-start | bytes 98312 | tf_op jit(solution)/shard_map/ppermute | solution.py:286
  53.4 4.6 %collective-permute-done.1 = f32[32,256]{1,0:T(8,128)S(1)} collective-permute-done((f32[32,256]{1,0:T(8,128)S(1)}, f32[32,256]{1,0:T(8,128)S(1)}, u32[]{:S(2)}, u32[]{:S(2)}) %collective-permute-start.1) | collective-permute-done | bytes 32800 | tf_op jit(solution)/shard_map/ppermute | solution.py:286
  58.0 0.0 collective-permute-done
  58.1 8.6 %all_to_all.17 = f32[4,96,256]{2,1,0:T(8,128)S(1)} all-to-all(f32[4,96,256]{2,1,0:T(8,128)S(1)} %broadcast_in_dim.6), channel_id=1, replica_groups=mesh['y'=4,'zh'=4,'zl'=4,'x'=4,'core'=2] {'x'}, dimensions={0} | all-to-all | bytes 786432 | tf_op jit(solution)/shard_map/all_to_all | solution.py:289
  66.7 5.9 %all-gather.2 = f32[8,96,256]{2,1,0:T(8,128)S(1)} all-gather(f32[4,96,256]{2,1,0:T(8,128)S(1)} %all_to_all.17), channel_id=4, replica_groups=mesh['y'=4,'zh'=4,'zl'=4,'x'=4,'core'=2] {'core'}, dimensions={0}, use_global_device_ids=true | all-gather | bytes 1179648 | tf_op jit(solution)/shard_map/all_gather | solution.py:289
  72.6 0.0 copy-start
  72.6 0.8 shard_map.50
  73.4 1.3 %collective-permute-start.2 = (f32[256,256]{1,0:T(8,128)S(1)}, f32[256,256]{1,0:T(8,128)S(1)}, u32[]{:S(2)}, u32[]{:S(2)}) collective-permute-start(f32[256,256]{1,0:T(8,128)S(1)} %get-tuple-element.13), channel_id=1, source_target_pairs={{128,0},{256,128},{384,256},{385,1},{130,2},{258,130},{386,258},{3... | collective-permute-start | bytes 786440 | tf_op jit(solution)/shard_map/ppermute | solution.py:293
  74.7 1.3 %collective-permute-start.3 = (f32[128,256]{1,0:T(8,128)S(1)}, f32[128,256]{1,0:T(8,128)S(1)}, u32[]{:S(2)}, u32[]{:S(2)}) collective-permute-start(f32[128,256]{1,0:T(8,128)S(1)} %get-tuple-element.14), channel_id=1, source_target_pairs={{256,0},{384,128},{257,1},{385,129},{258,2},{386,130},{259,3},{387... | collective-permute-start | bytes 393224 | tf_op jit(solution)/shard_map/ppermute | solution.py:294
  76.0 0.0 copy-done
  76.0 1.5 %shard_map.51.cur_ref = f32[256,256]{1,0:T(8,128)S(1)} custom-call(f32[2,4,136,128]{3,2,1,0:T(8,128)S(1)} %bitcast.11, f32[256,256]{1,0:T(8,128)S(1)} %bitcast.13), custom_call_target="tpu_custom_call" | custom-call | flops 402653184 | bytes 1081344 | tf_op jit(solution)/shard_map/pallas_call | solution.py:230
  77.5 0.9 %shard_map.52.cur_ref = f32[256,256]{1,0:T(8,128)S(1)} custom-call(f32[2,4,96,256]{3,2,1,0:T(8,128)S(1)} %bitcast.7, f32[256,256]{1,0:T(8,128)S(1)} %shard_map.51.cur_ref), custom_call_target="tpu_custom_call" | custom-call | flops 301989888 | bytes 1310720 | tf_op jit(solution)/shard_map/pallas_call | solution.py:230
  78.4 4.3 %collective-permute-done.3 = f32[128,256]{1,0:T(8,128)S(1)} collective-permute-done((f32[128,256]{1,0:T(8,128)S(1)}, f32[128,256]{1,0:T(8,128)S(1)}, u32[]{:S(2)}, u32[]{:S(2)}) %collective-permute-start.3) | collective-permute-done | bytes 131104 | tf_op jit(solution)/shard_map/ppermute | solution.py:294
  82.7 1.8 %collective-permute-done.2 = f32[256,256]{1,0:T(8,128)S(1)} collective-permute-done((f32[256,256]{1,0:T(8,128)S(1)}, f32[256,256]{1,0:T(8,128)S(1)}, u32[]{:S(2)}, u32[]{:S(2)}) %collective-permute-start.2) | collective-permute-done | bytes 262176 | tf_op jit(solution)/shard_map/ppermute | solution.py:293
  84.6 2.4 %all-gather.3 = f32[768,256]{1,0:T(8,128)S(1)} all-gather(f32[384,256]{1,0:T(8,128)S(1)} %pad_maximum_fusion), channel_id=5, replica_groups=mesh['y'=4,'zh'=4,'zl'=4,'x'=4,'core'=2] {'core'}, dimensions={0}, use_global_device_ids=true | all-gather | bytes 1179648 | tf_op jit(solution)/shard_map/all_gather | solution.py:295
  87.0 1.5 %shard_map.53 = f32[256,256]{1,0:T(8,128)} custom-call(f32[2,384,256]{2,1,0:T(8,128)S(1)} %bitcast.8, f32[256,256]{1,0:T(8,128)S(1)} %shard_map.52.cur_ref), custom_call_target="tpu_custom_call" | custom-call | flops 301989888 | bytes 1310720 | tf_op jit(solution)/shard_map/pallas_call | solution.py:230
  (5 shorter events, 0.1 us)
Async XLA Ops:
  39.2 18.8 %collective-permute-start = (f32[64,256]{1,0:T(8,128)S(1)}, f32[64,256]{1,0:T(8,128)S(1)}, u32[]{:S(2)}, u32[]{:S(2)}) collective-permute-start(f32[64,256]{1,0:T(8,128)S(1)} %get-tuple-element.10), channel_id=1, source_target_pairs={{0,96},{8,104},{16,112},{24,120},{32,0},{40,8},{48,16},{56,24},{64... | collective-permute-start | bytes 196616 | tf_op jit(solution)/shard_map/ppermute | solution.py:285
  47.2 10.8 %collective-permute-start.1 = (f32[32,256]{1,0:T(8,128)S(1)}, f32[32,256]{1,0:T(8,128)S(1)}, u32[]{:S(2)}, u32[]{:S(2)}) collective-permute-start(f32[32,256]{1,0:T(8,128)S(1)} %get-tuple-element.11), channel_id=1, source_target_pairs={{0,88},{8,80},{16,72},{24,64},{32,120},{40,112},{48,104},{56,96},{... | collective-permute-start | bytes 98312 | tf_op jit(solution)/shard_map/ppermute | solution.py:286
  72.6 3.4 %copy-start = (f32[1,256,256]{2,1,0:T(8,128)S(1)}, f32[1,256,256]{2,1,0:T(8,128)}, u32[]{:S(2)}) copy-start(f32[1,256,256]{2,1,0:T(8,128)} %param.4) | copy-start | bytes 786436
  73.4 11.1 %collective-permute-start.2 = (f32[256,256]{1,0:T(8,128)S(1)}, f32[256,256]{1,0:T(8,128)S(1)}, u32[]{:S(2)}, u32[]{:S(2)}) collective-permute-start(f32[256,256]{1,0:T(8,128)S(1)} %get-tuple-element.13), channel_id=1, source_target_pairs={{128,0},{256,128},{384,256},{385,1},{130,2},{258,130},{386,258},{3... | collective-permute-start | bytes 786440 | tf_op jit(solution)/shard_map/ppermute | solution.py:293
  74.7 8.0 %collective-permute-start.3 = (f32[128,256]{1,0:T(8,128)S(1)}, f32[128,256]{1,0:T(8,128)S(1)}, u32[]{:S(2)}, u32[]{:S(2)}) collective-permute-start(f32[128,256]{1,0:T(8,128)S(1)} %get-tuple-element.14), channel_id=1, source_target_pairs={{256,0},{384,128},{257,1},{385,129},{258,2},{386,130},{259,3},{387... | collective-permute-start | bytes 393224 | tf_op jit(solution)/shard_map/ppermute | solution.py:294

commit v5 on v4

--- a/solution.py
+++ b/solution.py
@@ -153,10 +153,10 @@
 
 
 def joined(ring_ref):
-    after = ring_ref[0, :, :WIDE].reshape(N, N)
-    before = ring_ref[1, :, :WIDE].reshape(N, N)
-    across = [ring_ref[core, :, WIDE:].reshape(H, N) for core in range(2)]
-    return after, jnp.concatenate(across, axis=0), before
+    across = ring_ref[0, :, :WIDE].reshape(N, N)
+    after = ring_ref[1, :, :WIDE].reshape(N, N)
+    before = [ring_ref[core, :, WIDE:].reshape(H, N) for core in range(2)]
+    return after, across, jnp.concatenate(before, axis=0)
 
 
 def ring_kernel(ring_ref, mine_ref, total_ref, half_ref, one, two):
@@ -241,12 +241,9 @@
 
 
 RING = 16
-NEAR = [
-    (2 * z + core, 2 * ((z + step) % RING) + core)
-    for core, step in enumerate((-4, 4))
-    for z in range(RING)
-]
-ACROSS = [(z, (11 - z) if z % 8 < 4 else (19 - z)) for z in range(RING)]
+ACROSS = [(2 * z, 2 * ((11 - z) if z % 8 < 4 else (19 - z))) for z in range(RING)]
+FIRST = ACROSS + [(2 * z + 1, 2 * ((z - 4) % RING) + 1) for z in range(RING)]
+BEFORE = [(z, (z + 4) % RING) for z in range(RING)]
 
 
 def from_later(steps):
@@ -282,9 +279,9 @@
     wide, thin = (WIDE, N), (THIN, N)
     total, wide, thin = call(quad_kernel, [full, wide, thin], (parts,), 3)
     current = call(quad_apply_kernel, full, (parts, current), 4)
-    near = lax.ppermute(wide, ("zh", "zl", "core"), NEAR)
-    across = lax.ppermute(thin, ("zh", "zl"), ACROSS)
-    piece = jnp.concatenate([near, across], axis=0)
+    first = lax.ppermute(wide, ("zh", "zl", "core"), FIRST)
+    before = lax.ppermute(thin, ("zh", "zl"), BEFORE)
+    piece = jnp.concatenate([first, before], axis=0)
     piece = jnp.broadcast_to(piece, (4, WIDE + THIN, N))
     ring = lax.all_gather(lax.all_to_all(piece, "x", 0, 0), "core")
     square = pltpu.VMEM(full, F32)

time: 89.1 us -> 89.2 us (level)
  starting transfers between devices: 16.7 us -> 13.4 us
  waiting for transfers between devices: 10.8 us -> 12.8 us
  blocking collectives: 51.4 us -> 53.1 us
    ppermute x2, starting transfers between devices: 14.1 us -> 10.9 us  [the longest x1 8.93 us: smoother(): first = lax.ppermute(wide, ('zh', 'zl', 'core'), FIRST)]
    ppermute x2, waiting for transfers between devices: 4.63 us -> 6.64 us  [the longest x1 6.64 us: smoother(): before = lax.ppermute(thin, ('zh', 'zl'), BEFORE)]
    all_gather x1, blocking collectives: 5.88 us -> 7.61 us  [smoother(): ring = lax.all_gather(lax.all_to_all(piece, 'x', 0, 0), 'core')]
where the time goes in v5:
time: 89.2 us; the launch traced here: 88.9 us
  blocking collectives  53.1 us (60%)
  starting transfers between devices  13.4 us (15%)
  waiting for transfers between devices  12.8 us (14%)
  Pallas kernels  9.32 us (10%)
    all_to_all x1, blocking collectives, smoother(): parts = lax.all_gather(lax.all_to_all(half, 'zl', 0, 0), 'core')  10.9 us
    pallas_call x8, Pallas kernels, call(): pl.pallas_call(kernel, out_shape=shapes if many else shapes[0], in_specs=...  9.32 us
    ppermute x1, starting transfers between devices, smoother(): first = lax.ppermute(wide, ('zh', 'zl', 'core'), FIRST)  8.93 us
    all_to_all x1, blocking collectives, smoother(): parts = lax.all_to_all(spread, 'x', 0, 0)  8.93 us
    all_to_all x1, blocking collectives, smoother(): ring = lax.all_gather(lax.all_to_all(piece, 'x', 0, 0), 'core')  8.62 us
    all_gather x1, blocking collectives, smoother(): both = lax.all_gather(gram, 'core')  8.48 us
    all_gather x1, blocking collectives, smoother(): ring = lax.all_gather(lax.all_to_all(piece, 'x', 0, 0), 'core')  7.61 us
    ppermute x1, waiting for transfers between devices, smoother(): before = lax.ppermute(thin, ('zh', 'zl'), BEFORE)  6.64 us
  transfers between devices with their start and end apart: 4, of which 3 were waited for; matrix products, arithmetic and copies ran while one was open for 0% of the time, Pallas kernels for 3%

profile of v5, /device:TPU:1, one launch (start us, length us, event | category | flops | bytes accessed | tf_op | source)
XLA Modules:
  0.0 88.9 jit_solution(8534867492834968890)
XLA Ops:
  0.0 1.8 %shard_map.46 = f32[272,128]{1,0:T(8,128)S(1)} custom-call(f32[256,256]{1,0:T(8,128)} %bitcast.12, f32[1,256]{1,0:T(1,128)} %refs_1_.1, s32[1,128]{1,0:T(1,128)} %refs_2_.1, f32[1,128]{1,0:T(1,128)} %refs_3_.1), custom_call_target="tpu_custom_call" | custom-call | flops 100663296 | bytes 403456 | tf_op jit(solution)/shard_map/pallas_call | solution.py:230
  1.8 8.5 %all-gather = f32[544,128]{1,0:T(8,128)S(1)} all-gather(f32[272,128]{1,0:T(8,128)S(1)} %shard_map.46), channel_id=2, replica_groups=mesh['y'=4,'zh'=4,'zl'=4,'x'=4,'core'=2] {'core'}, dimensions={0}, use_global_device_ids=true | all-gather | bytes 417792 | tf_op jit(solution)/shard_map/all_gather | solution.py:272
  10.3 8.9 %all_to_all.15 = f32[4,136,128]{2,1,0:T(8,128)S(1)} all-to-all(f32[4,136,128]{2,1,0:T(8,128)S(1)} %shard_map.47), channel_id=1, replica_groups=mesh['y'=4,'zh'=4,'zl'=4,'x'=4,'core'=2] {'x'}, dimensions={0} | all-to-all | bytes 557056 | tf_op jit(solution)/shard_map/all_to_all | solution.py:274
  19.2 2.8 %all_gather.30.halves_ref = f32[2,136,128]{2,1,0:T(8,128)S(1)} all-gather(f32[1,136,128]{2,1,0:T(8,128)S(1)} %fusion), channel_id=1, replica_groups=mesh['y'=4,'zh'=4,'zl'=4,'x'=4,'core'=2] {'core'}, dimensions={0}, use_global_device_ids=true | all-gather | bytes 208896 | tf_op jit(solution)/shard_map/all_gather | solution.py:275
  22.0 1.9 %shard_map.48 = f32[4,136,128]{2,1,0:T(8,128)S(1)} custom-call(f32[2,136,128]{2,1,0:T(8,128)S(1)} %all_gather.30.halves_ref), custom_call_target="tpu_custom_call" | custom-call | flops 603979776 | bytes 417792 | tf_op jit(solution)/shard_map/pallas_call | solution.py:230
  24.0 10.9 %all_to_all.16 = f32[4,136,128]{2,1,0:T(8,128)S(1)} all-to-all(f32[4,136,128]{2,1,0:T(8,128)S(1)} %shard_map.48), channel_id=1, replica_groups=mesh['y'=4,'zh'=4,'zl'=4,'x'=4,'core'=2] {'zl'}, dimensions={0} | all-to-all | bytes 557056 | tf_op jit(solution)/shard_map/all_to_all | solution.py:277
  34.9 3.5 %all-gather.1 = f32[8,136,128]{2,1,0:T(8,128)S(1)} all-gather(f32[4,136,128]{2,1,0:T(8,128)S(1)} %all_to_all.16), channel_id=3, replica_groups=mesh['y'=4,'zh'=4,'zl'=4,'x'=4,'core'=2] {'core'}, dimensions={0}, use_global_device_ids=true | all-gather | bytes 835584 | tf_op jit(solution)/shard_map/all_gather | solution.py:277
  38.3 0.9 %shard_map.49 = (f32[256,256]{1,0:T(8,128)S(1)}, f32[64,256]{1,0:T(8,128)S(1)}, f32[32,256]{1,0:T(8,128)S(1)}) custom-call(f32[2,4,136,128]{3,2,1,0:T(8,128)S(1)} %bitcast.10), custom_call_target="tpu_custom_call" | custom-call | flops 301989888 | bytes 917504 | tf_op jit(solution)/shard_map/pallas_call | solution.py:230
  39.2 8.9 %collective-permute-start = (f32[64,256]{1,0:T(8,128)S(1)}, f32[64,256]{1,0:T(8,128)S(1)}, u32[]{:S(2)}, u32[]{:S(2)}) collective-permute-start(f32[64,256]{1,0:T(8,128)S(1)} %get-tuple-element.10), channel_id=1, source_target_pairs={{0,88},{8,80},{16,72},{24,64},{32,120},{40,112},{48,104},{56,96},{... | collective-permute-start | bytes 196616 | tf_op jit(solution)/shard_map/ppermute | solution.py:282
  48.2 1.9 %collective-permute-start.1 = (f32[32,256]{1,0:T(8,128)S(1)}, f32[32,256]{1,0:T(8,128)S(1)}, u32[]{:S(2)}, u32[]{:S(2)}) collective-permute-start(f32[32,256]{1,0:T(8,128)S(1)} %get-tuple-element.11), channel_id=1, source_target_pairs={{0,32},{8,40},{16,48},{24,56},{32,64},{40,72},{48,80},{56,88},{64,... | collective-permute-start | bytes 98312 | tf_op jit(solution)/shard_map/ppermute | solution.py:283
  50.1 6.6 %collective-permute-done.1 = f32[32,256]{1,0:T(8,128)S(1)} collective-permute-done((f32[32,256]{1,0:T(8,128)S(1)}, f32[32,256]{1,0:T(8,128)S(1)}, u32[]{:S(2)}, u32[]{:S(2)}) %collective-permute-start.1) | collective-permute-done | bytes 32800 | tf_op jit(solution)/shard_map/ppermute | solution.py:283
  56.7 0.0 collective-permute-done
  56.8 8.6 %all_to_all.17 = f32[4,96,256]{2,1,0:T(8,128)S(1)} all-to-all(f32[4,96,256]{2,1,0:T(8,128)S(1)} %broadcast_in_dim.6), channel_id=1, replica_groups=mesh['y'=4,'zh'=4,'zl'=4,'x'=4,'core'=2] {'x'}, dimensions={0} | all-to-all | bytes 786432 | tf_op jit(solution)/shard_map/all_to_all | solution.py:286
  65.4 7.6 %all-gather.2 = f32[8,96,256]{2,1,0:T(8,128)S(1)} all-gather(f32[4,96,256]{2,1,0:T(8,128)S(1)} %all_to_all.17), channel_id=4, replica_groups=mesh['y'=4,'zh'=4,'zl'=4,'x'=4,'core'=2] {'core'}, dimensions={0}, use_global_device_ids=true | all-gather | bytes 1179648 | tf_op jit(solution)/shard_map/all_gather | solution.py:286
  73.0 0.0 copy-start
  73.0 0.8 shard_map.50
  73.9 1.3 %collective-permute-start.2 = (f32[256,256]{1,0:T(8,128)S(1)}, f32[256,256]{1,0:T(8,128)S(1)}, u32[]{:S(2)}, u32[]{:S(2)}) collective-permute-start(f32[256,256]{1,0:T(8,128)S(1)} %get-tuple-element.13), channel_id=1, source_target_pairs={{128,0},{256,128},{384,256},{385,1},{130,2},{258,130},{386,258},{3... | collective-permute-start | bytes 786440 | tf_op jit(solution)/shard_map/ppermute | solution.py:290
  75.2 1.3 %collective-permute-start.3 = (f32[128,256]{1,0:T(8,128)S(1)}, f32[128,256]{1,0:T(8,128)S(1)}, u32[]{:S(2)}, u32[]{:S(2)}) collective-permute-start(f32[128,256]{1,0:T(8,128)S(1)} %get-tuple-element.14), channel_id=1, source_target_pairs={{256,0},{384,128},{257,1},{385,129},{258,2},{386,130},{259,3},{387... | collective-permute-start | bytes 393224 | tf_op jit(solution)/shard_map/ppermute | solution.py:291
  76.5 0.0 copy-done
  76.5 1.5 %shard_map.51.cur_ref = f32[256,256]{1,0:T(8,128)S(1)} custom-call(f32[2,4,136,128]{3,2,1,0:T(8,128)S(1)} %bitcast.11, f32[256,256]{1,0:T(8,128)S(1)} %bitcast.13), custom_call_target="tpu_custom_call" | custom-call | flops 402653184 | bytes 1081344 | tf_op jit(solution)/shard_map/pallas_call | solution.py:230
  78.0 0.9 %shard_map.52.cur_ref = f32[256,256]{1,0:T(8,128)S(1)} custom-call(f32[2,4,96,256]{3,2,1,0:T(8,128)S(1)} %bitcast.7, f32[256,256]{1,0:T(8,128)S(1)} %shard_map.51.cur_ref), custom_call_target="tpu_custom_call" | custom-call | flops 301989888 | bytes 1310720 | tf_op jit(solution)/shard_map/pallas_call | solution.py:230
  78.9 4.3 %collective-permute-done.3 = f32[128,256]{1,0:T(8,128)S(1)} collective-permute-done((f32[128,256]{1,0:T(8,128)S(1)}, f32[128,256]{1,0:T(8,128)S(1)}, u32[]{:S(2)}, u32[]{:S(2)}) %collective-permute-start.3) | collective-permute-done | bytes 131104 | tf_op jit(solution)/shard_map/ppermute | solution.py:291
  83.2 1.8 %collective-permute-done.2 = f32[256,256]{1,0:T(8,128)S(1)} collective-permute-done((f32[256,256]{1,0:T(8,128)S(1)}, f32[256,256]{1,0:T(8,128)S(1)}, u32[]{:S(2)}, u32[]{:S(2)}) %collective-permute-start.2) | collective-permute-done | bytes 262176 | tf_op jit(solution)/shard_map/ppermute | solution.py:290
  85.0 2.4 %all-gather.3 = f32[768,256]{1,0:T(8,128)S(1)} all-gather(f32[384,256]{1,0:T(8,128)S(1)} %pad_maximum_fusion), channel_id=5, replica_groups=mesh['y'=4,'zh'=4,'zl'=4,'x'=4,'core'=2] {'core'}, dimensions={0}, use_global_device_ids=true | all-gather | bytes 1179648 | tf_op jit(solution)/shard_map/all_gather | solution.py:292
  87.4 1.5 %shard_map.53 = f32[256,256]{1,0:T(8,128)} custom-call(f32[2,384,256]{2,1,0:T(8,128)S(1)} %bitcast.8, f32[256,256]{1,0:T(8,128)S(1)} %shard_map.52.cur_ref), custom_call_target="tpu_custom_call" | custom-call | flops 301989888 | bytes 1310720 | tf_op jit(solution)/shard_map/pallas_call | solution.py:230
  (5 shorter events, 0.1 us)
Async XLA Ops:
  39.2 17.5 %collective-permute-start = (f32[64,256]{1,0:T(8,128)S(1)}, f32[64,256]{1,0:T(8,128)S(1)}, u32[]{:S(2)}, u32[]{:S(2)}) collective-permute-start(f32[64,256]{1,0:T(8,128)S(1)} %get-tuple-element.10), channel_id=1, source_target_pairs={{0,88},{8,80},{16,72},{24,64},{32,120},{40,112},{48,104},{56,96},{... | collective-permute-start | bytes 196616 | tf_op jit(solution)/shard_map/ppermute | solution.py:282
  48.2 8.6 %collective-permute-start.1 = (f32[32,256]{1,0:T(8,128)S(1)}, f32[32,256]{1,0:T(8,128)S(1)}, u32[]{:S(2)}, u32[]{:S(2)}) collective-permute-start(f32[32,256]{1,0:T(8,128)S(1)} %get-tuple-element.11), channel_id=1, source_target_pairs={{0,32},{8,40},{16,48},{24,56},{32,64},{40,72},{48,80},{56,88},{64,... | collective-permute-start | bytes 98312 | tf_op jit(solution)/shard_map/ppermute | solution.py:283
  73.0 3.4 %copy-start = (f32[1,256,256]{2,1,0:T(8,128)S(1)}, f32[1,256,256]{2,1,0:T(8,128)}, u32[]{:S(2)}) copy-start(f32[1,256,256]{2,1,0:T(8,128)} %param.4) | copy-start | bytes 786436
  73.9 11.1 %collective-permute-start.2 = (f32[256,256]{1,0:T(8,128)S(1)}, f32[256,256]{1,0:T(8,128)S(1)}, u32[]{:S(2)}, u32[]{:S(2)}) collective-permute-start(f32[256,256]{1,0:T(8,128)S(1)} %get-tuple-element.13), channel_id=1, source_target_pairs={{128,0},{256,128},{384,256},{385,1},{130,2},{258,130},{386,258},{3... | collective-permute-start | bytes 786440 | tf_op jit(solution)/shard_map/ppermute | solution.py:290
  75.2 8.0 %collective-permute-start.3 = (f32[128,256]{1,0:T(8,128)S(1)}, f32[128,256]{1,0:T(8,128)S(1)}, u32[]{:S(2)}, u32[]{:S(2)}) collective-permute-start(f32[128,256]{1,0:T(8,128)S(1)} %get-tuple-element.14), channel_id=1, source_target_pairs={{256,0},{384,128},{257,1},{385,129},{258,2},{386,130},{259,3},{387... | collective-permute-start | bytes 393224 | tf_op jit(solution)/shard_map/ppermute | solution.py:291

commit v6 on v4

--- a/solution.py
+++ b/solution.py
@@ -70,12 +70,15 @@
     ]
     for copy in copies:
         copy.start()
-    for copy in copies:
+    cur_ref, mean_ref, rows_ref, prec_ref = held
+    for copy in copies[1:]:
         copy.wait()
-    cur_ref, mean_ref, rows_ref, prec_ref = held
-    value = cur_ref[...] + column(mean_ref[...], N)
+    mean = column(mean_ref[...], N)
+    weight = jnp.sqrt(column(prec_ref[...], H))
     state_row = lax.broadcasted_iota(jnp.int32, (N, H), 0)
     chosen = (state_row == rows_ref[...]).astype(F32).T.astype(BF16)
+    copies[0].wait()
+    value = cur_ref[...] + mean
     dot = functools.partial(jnp.dot, preferred_element_type=F32)
     one = value.astype(BF16)
     rest = value - one.astype(F32)
@@ -84,7 +87,7 @@
     picked = dot(chosen, one) + (dot(chosen, two) + dot(chosen, three))
     predicted = jnp.tanh(picked)
     centred = predicted - jnp.mean(predicted, axis=1, keepdims=True)
-    centred = centred * jnp.sqrt(column(prec_ref[...], H))
+    centred = centred * weight
     gram = mm(split(centred.T), split(centred)) * (1.0 / (N - 1))
     pack(gram, out_ref)
 

time: 89.1 us -> 89 us (level)
  no operation moved by 1% of the time
where the time goes in v6:
time: 89 us; the launch traced here: 88.3 us
  blocking collectives  51.4 us (58%)
  starting transfers between devices  16.7 us (19%)
  waiting for transfers between devices  10.8 us (12%)
  Pallas kernels  9.23 us (10%)
    all_to_all x1, blocking collectives, smoother(): parts = lax.all_gather(lax.all_to_all(half, 'zl', 0, 0), 'core')  10.9 us
    pallas_call x8, Pallas kernels, call(): pl.pallas_call(kernel, out_shape=shapes if many else shapes[0], in_specs=...  9.23 us
    all_to_all x1, blocking collectives, smoother(): parts = lax.all_to_all(spread, 'x', 0, 0)  8.93 us
    all_to_all x1, blocking collectives, smoother(): ring = lax.all_gather(lax.all_to_all(piece, 'x', 0, 0), 'core')  8.62 us
    all_gather x1, blocking collectives, smoother(): both = lax.all_gather(gram, 'core')  8.48 us
    ppermute x1, starting transfers between devices, smoother(): near = lax.ppermute(wide, ('zh', 'zl', 'core'), NEAR)  7.99 us
    ppermute x1, starting transfers between devices, smoother(): across = lax.ppermute(thin, ('zh', 'zl'), ACROSS)  6.14 us
    all_gather x1, blocking collectives, smoother(): ring = lax.all_gather(lax.all_to_all(piece, 'x', 0, 0), 'core')  5.88 us
  transfers between devices with their start and end apart: 4, of which 3 were waited for; matrix products, arithmetic and copies ran while one was open for 0% of the time, Pallas kernels for 3%

profile of v6, /device:TPU:1, one launch (start us, length us, event | category | flops | bytes accessed | tf_op | source)
XLA Modules:
  0.0 88.3 jit_solution(16823571584350203977)
XLA Ops:
  0.0 1.7 %shard_map.46 = f32[272,128]{1,0:T(8,128)S(1)} custom-call(f32[256,256]{1,0:T(8,128)} %bitcast.12, f32[1,256]{1,0:T(1,128)} %refs_1_.1, s32[1,128]{1,0:T(1,128)} %refs_2_.1, f32[1,128]{1,0:T(1,128)} %refs_3_.1), custom_call_target="tpu_custom_call" | custom-call | flops 100663296 | bytes 403456 | tf_op jit(solution)/shard_map/pallas_call | solution.py:233
  1.7 8.5 %all-gather = f32[544,128]{1,0:T(8,128)S(1)} all-gather(f32[272,128]{1,0:T(8,128)S(1)} %shard_map.46), channel_id=2, replica_groups=mesh['y'=4,'zh'=4,'zl'=4,'x'=4,'core'=2] {'core'}, dimensions={0}, use_global_device_ids=true | all-gather | bytes 417792 | tf_op jit(solution)/shard_map/all_gather | solution.py:278
  10.2 8.9 %all_to_all.15 = f32[4,136,128]{2,1,0:T(8,128)S(1)} all-to-all(f32[4,136,128]{2,1,0:T(8,128)S(1)} %shard_map.47), channel_id=1, replica_groups=mesh['y'=4,'zh'=4,'zl'=4,'x'=4,'core'=2] {'x'}, dimensions={0} | all-to-all | bytes 557056 | tf_op jit(solution)/shard_map/all_to_all | solution.py:280
  19.2 2.8 %all_gather.30.halves_ref = f32[2,136,128]{2,1,0:T(8,128)S(1)} all-gather(f32[1,136,128]{2,1,0:T(8,128)S(1)} %fusion), channel_id=1, replica_groups=mesh['y'=4,'zh'=4,'zl'=4,'x'=4,'core'=2] {'core'}, dimensions={0}, use_global_device_ids=true | all-gather | bytes 208896 | tf_op jit(solution)/shard_map/all_gather | solution.py:281
  21.9 1.9 %shard_map.48 = f32[4,136,128]{2,1,0:T(8,128)S(1)} custom-call(f32[2,136,128]{2,1,0:T(8,128)S(1)} %all_gather.30.halves_ref), custom_call_target="tpu_custom_call" | custom-call | flops 603979776 | bytes 417792 | tf_op jit(solution)/shard_map/pallas_call | solution.py:233
  23.9 10.9 %all_to_all.16 = f32[4,136,128]{2,1,0:T(8,128)S(1)} all-to-all(f32[4,136,128]{2,1,0:T(8,128)S(1)} %shard_map.48), channel_id=1, replica_groups=mesh['y'=4,'zh'=4,'zl'=4,'x'=4,'core'=2] {'zl'}, dimensions={0} | all-to-all | bytes 557056 | tf_op jit(solution)/shard_map/all_to_all | solution.py:283
  34.8 3.5 %all-gather.1 = f32[8,136,128]{2,1,0:T(8,128)S(1)} all-gather(f32[4,136,128]{2,1,0:T(8,128)S(1)} %all_to_all.16), channel_id=3, replica_groups=mesh['y'=4,'zh'=4,'zl'=4,'x'=4,'core'=2] {'core'}, dimensions={0}, use_global_device_ids=true | all-gather | bytes 835584 | tf_op jit(solution)/shard_map/all_gather | solution.py:283
  38.2 0.9 %shard_map.49 = (f32[256,256]{1,0:T(8,128)S(1)}, f32[64,256]{1,0:T(8,128)S(1)}, f32[32,256]{1,0:T(8,128)S(1)}) custom-call(f32[2,4,136,128]{3,2,1,0:T(8,128)S(1)} %bitcast.10), custom_call_target="tpu_custom_call" | custom-call | flops 301989888 | bytes 917504 | tf_op jit(solution)/shard_map/pallas_call | solution.py:233
  39.2 8.0 %collective-permute-start = (f32[64,256]{1,0:T(8,128)S(1)}, f32[64,256]{1,0:T(8,128)S(1)}, u32[]{:S(2)}, u32[]{:S(2)}) collective-permute-start(f32[64,256]{1,0:T(8,128)S(1)} %get-tuple-element.10), channel_id=1, source_target_pairs={{0,96},{8,104},{16,112},{24,120},{32,0},{40,8},{48,16},{56,24},{64... | collective-permute-start | bytes 196616 | tf_op jit(solution)/shard_map/ppermute | solution.py:288
  47.2 6.1 %collective-permute-start.1 = (f32[32,256]{1,0:T(8,128)S(1)}, f32[32,256]{1,0:T(8,128)S(1)}, u32[]{:S(2)}, u32[]{:S(2)}) collective-permute-start(f32[32,256]{1,0:T(8,128)S(1)} %get-tuple-element.11), channel_id=1, source_target_pairs={{0,88},{8,80},{16,72},{24,64},{32,120},{40,112},{48,104},{56,96},{... | collective-permute-start | bytes 98312 | tf_op jit(solution)/shard_map/ppermute | solution.py:289
  53.3 4.6 %collective-permute-done.1 = f32[32,256]{1,0:T(8,128)S(1)} collective-permute-done((f32[32,256]{1,0:T(8,128)S(1)}, f32[32,256]{1,0:T(8,128)S(1)}, u32[]{:S(2)}, u32[]{:S(2)}) %collective-permute-start.1) | collective-permute-done | bytes 32800 | tf_op jit(solution)/shard_map/ppermute | solution.py:289
  57.9 0.0 collective-permute-done
  58.0 8.6 %all_to_all.17 = f32[4,96,256]{2,1,0:T(8,128)S(1)} all-to-all(f32[4,96,256]{2,1,0:T(8,128)S(1)} %broadcast_in_dim.6), channel_id=1, replica_groups=mesh['y'=4,'zh'=4,'zl'=4,'x'=4,'core'=2] {'x'}, dimensions={0} | all-to-all | bytes 786432 | tf_op jit(solution)/shard_map/all_to_all | solution.py:292
  66.6 5.9 %all-gather.2 = f32[8,96,256]{2,1,0:T(8,128)S(1)} all-gather(f32[4,96,256]{2,1,0:T(8,128)S(1)} %all_to_all.17), channel_id=4, replica_groups=mesh['y'=4,'zh'=4,'zl'=4,'x'=4,'core'=2] {'core'}, dimensions={0}, use_global_device_ids=true | all-gather | bytes 1179648 | tf_op jit(solution)/shard_map/all_gather | solution.py:292
  72.5 0.0 copy-start
  72.5 0.8 shard_map.50
  73.3 1.3 %collective-permute-start.2 = (f32[256,256]{1,0:T(8,128)S(1)}, f32[256,256]{1,0:T(8,128)S(1)}, u32[]{:S(2)}, u32[]{:S(2)}) collective-permute-start(f32[256,256]{1,0:T(8,128)S(1)} %get-tuple-element.13), channel_id=1, source_target_pairs={{128,0},{256,128},{384,256},{385,1},{130,2},{258,130},{386,258},{3... | collective-permute-start | bytes 786440 | tf_op jit(solution)/shard_map/ppermute | solution.py:296
  74.6 1.3 %collective-permute-start.3 = (f32[128,256]{1,0:T(8,128)S(1)}, f32[128,256]{1,0:T(8,128)S(1)}, u32[]{:S(2)}, u32[]{:S(2)}) collective-permute-start(f32[128,256]{1,0:T(8,128)S(1)} %get-tuple-element.14), channel_id=1, source_target_pairs={{256,0},{384,128},{257,1},{385,129},{258,2},{386,130},{259,3},{387... | collective-permute-start | bytes 393224 | tf_op jit(solution)/shard_map/ppermute | solution.py:297
  75.9 0.0 copy-done
  75.9 1.5 %shard_map.51.cur_ref = f32[256,256]{1,0:T(8,128)S(1)} custom-call(f32[2,4,136,128]{3,2,1,0:T(8,128)S(1)} %bitcast.11, f32[256,256]{1,0:T(8,128)S(1)} %bitcast.13), custom_call_target="tpu_custom_call" | custom-call | flops 402653184 | bytes 1081344 | tf_op jit(solution)/shard_map/pallas_call | solution.py:233
  77.4 0.9 %shard_map.52.cur_ref = f32[256,256]{1,0:T(8,128)S(1)} custom-call(f32[2,4,96,256]{3,2,1,0:T(8,128)S(1)} %bitcast.7, f32[256,256]{1,0:T(8,128)S(1)} %shard_map.51.cur_ref), custom_call_target="tpu_custom_call" | custom-call | flops 301989888 | bytes 1310720 | tf_op jit(solution)/shard_map/pallas_call | solution.py:233
  78.3 4.3 %collective-permute-done.3 = f32[128,256]{1,0:T(8,128)S(1)} collective-permute-done((f32[128,256]{1,0:T(8,128)S(1)}, f32[128,256]{1,0:T(8,128)S(1)}, u32[]{:S(2)}, u32[]{:S(2)}) %collective-permute-start.3) | collective-permute-done | bytes 131104 | tf_op jit(solution)/shard_map/ppermute | solution.py:297
  82.6 1.8 %collective-permute-done.2 = f32[256,256]{1,0:T(8,128)S(1)} collective-permute-done((f32[256,256]{1,0:T(8,128)S(1)}, f32[256,256]{1,0:T(8,128)S(1)}, u32[]{:S(2)}, u32[]{:S(2)}) %collective-permute-start.2) | collective-permute-done | bytes 262176 | tf_op jit(solution)/shard_map/ppermute | solution.py:296
  84.5 2.4 %all-gather.3 = f32[768,256]{1,0:T(8,128)S(1)} all-gather(f32[384,256]{1,0:T(8,128)S(1)} %pad_maximum_fusion), channel_id=5, replica_groups=mesh['y'=4,'zh'=4,'zl'=4,'x'=4,'core'=2] {'core'}, dimensions={0}, use_global_device_ids=true | all-gather | bytes 1179648 | tf_op jit(solution)/shard_map/all_gather | solution.py:298
  86.9 1.5 %shard_map.53 = f32[256,256]{1,0:T(8,128)} custom-call(f32[2,384,256]{2,1,0:T(8,128)S(1)} %bitcast.8, f32[256,256]{1,0:T(8,128)S(1)} %shard_map.52.cur_ref), custom_call_target="tpu_custom_call" | custom-call | flops 301989888 | bytes 1310720 | tf_op jit(solution)/shard_map/pallas_call | solution.py:233
  (5 shorter events, 0.1 us)
Async XLA Ops:
  39.2 18.8 %collective-permute-start = (f32[64,256]{1,0:T(8,128)S(1)}, f32[64,256]{1,0:T(8,128)S(1)}, u32[]{:S(2)}, u32[]{:S(2)}) collective-permute-start(f32[64,256]{1,0:T(8,128)S(1)} %get-tuple-element.10), channel_id=1, source_target_pairs={{0,96},{8,104},{16,112},{24,120},{32,0},{40,8},{48,16},{56,24},{64... | collective-permute-start | bytes 196616 | tf_op jit(solution)/shard_map/ppermute | solution.py:288
  47.2 10.8 %collective-permute-start.1 = (f32[32,256]{1,0:T(8,128)S(1)}, f32[32,256]{1,0:T(8,128)S(1)}, u32[]{:S(2)}, u32[]{:S(2)}) collective-permute-start(f32[32,256]{1,0:T(8,128)S(1)} %get-tuple-element.11), channel_id=1, source_target_pairs={{0,88},{8,80},{16,72},{24,64},{32,120},{40,112},{48,104},{56,96},{... | collective-permute-start | bytes 98312 | tf_op jit(solution)/shard_map/ppermute | solution.py:289
  72.5 3.4 %copy-start = (f32[1,256,256]{2,1,0:T(8,128)S(1)}, f32[1,256,256]{2,1,0:T(8,128)}, u32[]{:S(2)}) copy-start(f32[1,256,256]{2,1,0:T(8,128)} %param.4) | copy-start | bytes 786436
  73.3 11.1 %collective-permute-start.2 = (f32[256,256]{1,0:T(8,128)S(1)}, f32[256,256]{1,0:T(8,128)S(1)}, u32[]{:S(2)}, u32[]{:S(2)}) collective-permute-start(f32[256,256]{1,0:T(8,128)S(1)} %get-tuple-element.13), channel_id=1, source_target_pairs={{128,0},{256,128},{384,256},{385,1},{130,2},{258,130},{386,258},{3... | collective-permute-start | bytes 786440 | tf_op jit(solution)/shard_map/ppermute | solution.py:296
  74.6 8.0 %collective-permute-start.3 = (f32[128,256]{1,0:T(8,128)S(1)}, f32[128,256]{1,0:T(8,128)S(1)}, u32[]{:S(2)}, u32[]{:S(2)}) collective-permute-start(f32[128,256]{1,0:T(8,128)S(1)} %get-tuple-element.14), channel_id=1, source_target_pairs={{256,0},{384,128},{257,1},{385,129},{258,2},{386,130},{259,3},{387... | collective-permute-start | bytes 393224 | tf_op jit(solution)/shard_map/ppermute | solution.py:297
